TPU v7x, 512 devices: a whole 4x8x8 slice. The times are simulated.
512 devices in a mesh: tiles: 64 (over y, x, core), pix: 8 (over z).
Axes of the slice: x: 4, y: 8, z: 8, core: 2. Of those that a mesh axis runs over, the one named last changes fastest.
Arguments:
- frames: bfloat16 [16384, 32768], P('tiles', 'pix'), may hold values from -60 to 60
- tile_valid: int32 [16384], P('tiles'), may hold values from 0 to 1
- foreground_blocks: int32 [16384], P('tiles'), may hold values from 0 to 8, as said below
- basis_start: float32 [16, 32768], P(None, 'pix'), may hold values from -12 to 12
- dark_start: float32 [32768], P('pix'), may hold values from -4 to 4
Outputs:
- flatfield_basis: float32 [16, 32768], P(None, 'pix')
- darkfield: float32 [32768], P('pix')
- coefficients: float32 [16384, 16], P('tiles')
Inputs may be any that keep to these rules, and one draw needn't show every extreme that they name: `foreground_blocks`: some tile has exactly 8.
All inputs are finite; a program needn't handle non-finite values.
Results may differ from a plain program's by a relative error of at most 0.0003.
Values sent between devices are 32-bit elements; how exact they have to be, the bound alone decides.
A program may use at most 64 MiB of HBM per device.

v0:
```python
import jax
import jax.numpy as jnp
from jax import lax
from jax.sharding import Mesh
from jax.sharding import PartitionSpec as P

ROW_PX = 2048
ITERS = 2
TILES = ("tiles_0", "tiles_1", "tiles_2")


precise = lax.Precision.HIGHEST
ridge_weight = 0.01


def sent_to_all(x, axis):
    length = lax.axis_size(axis)
    return lax.all_to_all(jnp.broadcast_to(x[None], (length, *x.shape)), axis, 0, 0, tiled=True)


def taken_together(x, axis):
    return sent_to_all(x, axis).sum(axis=0)


def over_axes(x, axes):
    far, near = axes
    return taken_together(taken_together(x, near), far)


def filled_up(lines, length):
    spare = -lines.shape[0] % length
    if not spare:
        return lines
    return jnp.concatenate([lines, jnp.zeros((spare, *lines.shape[1:]), lines.dtype)])


def in_order(pieces, dim):
    lengths = list(pieces.shape[1:])
    lengths[dim] *= pieces.shape[0]
    return jnp.moveaxis(pieces, 0, dim).reshape(lengths)


def whole_of(x, axes, dim):
    far, near = axes
    initial = sent_to_all(x, far)
    pieces = jnp.swapaxes(sent_to_all(initial, near), 0, 1)
    return in_order(pieces.reshape(-1, *x.shape), dim)


def split_up(x, dim, length):
    lengths = x.shape
    pieces = x.reshape(*lengths[:dim], length, lengths[dim] // length, *lengths[dim + 1 :])
    return jnp.moveaxis(pieces, dim, 0)


def sent_and_summed(x, axis, dim):
    length = lax.axis_size(axis)
    pieces = lax.all_to_all(split_up(x, dim, length), axis, 0, 0, tiled=True)
    return jnp.sum(pieces, axis=0)


def summed_rows(x, axes, dim):
    far, near = axes
    pieces = split_up(x, dim, lax.axis_size(far))
    nearer = sent_and_summed(pieces, near, dim + 1)
    arrived = lax.all_to_all(nearer, far, split_axis=0, concat_axis=0, tiled=True)
    return arrived.sum(axis=0)


def nested_sum(x, axes):
    lines = x.reshape(-1)
    padded = filled_up(lines, lax.axis_size(axes[0]) * lax.axis_size(axes[1]))
    whole = whole_of(summed_rows(padded, axes, 0), axes, 0)
    return lax.slice_in_dim(whole, 0, len(lines)).reshape(x.shape)


def solve_gram(gram_matrix, right_rows):
    factor = jnp.linalg.cholesky(gram_matrix)
    return jax.scipy.linalg.cho_solve((factor, True), right_rows)


def advance(basis, darkfield, totals, gram_c, tile_count):
    components = basis.shape[0]
    change = solve_gram(gram_c, totals[:components] / tile_count)
    return (basis + change, darkfield + totals[components] / (totals[components + 1] + 1.0))


def local(frames, tile_valid, foreground_blocks, basis_start, dark_start):
    tile_dev, pix_dev = frames.shape
    components = basis_start.shape[0]
    tiles_all = tile_dev * lax.axis_size(TILES)
    pixels_all = pix_dev * lax.axis_size("pix")
    column = jnp.arange(pix_dev, dtype=jnp.int32) % ROW_PX // 128
    valid_float = tile_valid.astype(jnp.float32)
    usable = valid_float[:, None] * (column[None, :] >= foreground_blocks[:, None]).astype(
        jnp.float32
    )
    identity = jnp.eye(components, dtype=jnp.float32)
    basis = basis_start
    darkfield = dark_start
    coefficients = jnp.zeros((tile_dev, components), jnp.float32)
    for iteration in range(ITERS):
        shifted = frames.astype(jnp.float32) - darkfield[None, :]
        local_gram = jnp.dot(basis, basis.T, precision=precise)
        local_proj = jnp.dot(shifted, basis.T, precision=precise)
        gram_total, proj_total = (
            taken_together(local_gram, "pix"),
            taken_together(local_proj, "pix"),
        )
        gram_f = gram_total / pixels_all + ridge_weight * identity
        coefficients = solve_gram(gram_f, (proj_total / pixels_all).T).T
        residual = shifted - jnp.dot(coefficients, basis, precision=precise)
        local_square = jnp.sum(usable * residual * residual)
        local_coef_gram = jnp.dot(
            (coefficients * valid_float[:, None]).T, coefficients, precision=precise
        )
        square_total = over_axes(local_square, (("tiles_0", "tiles_1"), ("tiles_2", "pix")))
        coef_total = taken_together(local_coef_gram, TILES)
        spread = square_total / (tiles_all * pixels_all) + 1e-05
        weights = usable / (1.0 + residual * residual / (4.0 * spread))
        weighted = weights * residual
        column_terms = jnp.concatenate(
            [
                jnp.dot(coefficients.T, weighted, precision=precise),
                jnp.sum(weighted, axis=0, keepdims=True),
                jnp.sum(weights, axis=0, keepdims=True),
            ],
            axis=0,
        )
        gram_c = coef_total / tiles_all + ridge_weight * identity
        totals = nested_sum(column_terms, (("tiles_0", "tiles_1"), "tiles_2"))
        basis, darkfield = advance(basis, darkfield, totals, gram_c, tiles_all)
    return (basis, darkfield, coefficients)


def solution(mesh):
    finer = Mesh(
        mesh.devices.reshape(8, 4, 2, mesh.shape["pix"]), ("tiles_0", "tiles_1", "tiles_2", "pix")
    )
    in_specs = (P(TILES, "pix"), P(TILES), P(TILES), P(None, "pix"), P("pix"))
    out_specs = (P(None, "pix"), P("pix"), P(TILES, None))
    return jax.shard_map(local, mesh=finer, in_specs=in_specs, out_specs=out_specs, check_vma=False)
```

profile of v0, /device:TPU:1, one launch (start us, length us, event | category | flops | bytes accessed | tf_op | source)
XLA Modules:
  0.0 262.1 jit_solution(3820560281964582881)
XLA Ops:
  0.6 1.5 fusion.62
  2.1 0.7 reshape.93
  2.8 10.8 %all-to-all-start = ((f32[8,1,256]{2,1,0:T(1,128)}), f32[8,1,256]{2,1,0:T(1,128)S(1)}, u32[]{:S(2)}, u32[]{:S(2)}) async-start(f32[8,1,256]{2,1,0:T(1,128)} %reshape.93), calls=%async_computation | async-start | bytes 16384 | tf_op jit(solution)/shard_map/all_to_all | solution.py:18
  13.7 5.0 %fusion.2 = f32[256,16]{0,1:T(8,128)S(1)} fusion(f32[16,4096]{1,0:T(8,128)} %param.13, bf16[256,4096]{1,0:T(8,128)(2,1)} %param.10, f32[4096]{0:T(1024)} %param.14), kind=kOutput, calls=%fused_computation.10 | convolution fusion | flops 203423744 | bytes 2392064 | tf_op jit(solution)/shard_map/dot_general | solution.py:105
  18.7 0.7 convert_element_type.10
  19.4 0.9 all-to-all-done
  20.3 0.7 broadcast_in_dim.42
  20.9 5.8 %all-to-all-start.1 = ((f32[8,256,16]{1,2,0:T(8,128)}), f32[8,256,16]{1,2,0:T(8,128)S(1)}, u32[]{:S(2)}, u32[]{:S(2)}) async-start(f32[8,256,16]{1,2,0:T(8,128)} %broadcast_in_dim.42), calls=%async_computation.1 | async-start | bytes 262144 | tf_op jit(solution)/shard_map/all_to_all | solution.py:18
  28.0 1.5 cholesky.74
  30.2 0.6 fusion.34
  30.8 1.2 custom-call.14
  32.1 2.6 all-to-all-done.1
  35.0 7.8 %fusion.5 = (f32[]{:T(128)}, f32[256,4096]{1,0:T(8,128)}) fusion(f32[256]{0:T(256)S(1)} %convert_element_type.10, s32[4096]{0:T(1024)S(1)} %add_select_fusion, s32[256]{0:T(256)} %param.12, f32[16,256]{1,0:T(8,128)S(1)} %fusion.48, f32[16,4096]{1,0:T(8,128)} %param.13, f32[4096]{0:T(1024)} %param.14, bf16[256,4096]{1,0:T(8,128)(2,1)} %param.10), kind=kOutput, calls=%fused_computation.15 | convolution fusion | flops 209715200 | bytes 6604804 | tf_op jit(solution)/shard_map/dot_general | solution.py:112
  43.5 13.0 %all_to_all.104 = f32[16,1,1]{2,1,0:T(1,128)S(1)} all-to-all(f32[16,1,1]{2,1,0:T(1,128)S(1)} %broadcast_in_dim.44), channel_id=1, replica_groups=mesh['tiles_0'=8,'tiles_1'=4,'tiles_2'=2,'pix'=8] {'tiles_2','pix'}, dimensions={0} | all-to-all | bytes 128 | tf_op jit(solution)/shard_map/all_to_all | solution.py:18
  57.1 1.3 broadcast_in_dim.45
  58.3 9.7 %all-to-all-start.4 = ((f32[32,1,1]{2,1,0:T(1,128)}), f32[32,1,1]{2,1,0:T(1,128)S(1)}, u32[]{:S(2)}, u32[]{:S(2)}) async-start(f32[32,1,1]{2,1,0:T(1,128)} %broadcast_in_dim.45), calls=%async_computation.4 | async-start | bytes 32768 | tf_op jit(solution)/shard_map/all_to_all | solution.py:18
  68.2 0.9 reshape.95
  69.0 7.5 %all-to-all-done.4 = f32[32,1,1]{2,1,0:T(1,128)S(1)} async-done(((f32[32,1,1]{2,1,0:T(1,128)}), f32[32,1,1]{2,1,0:T(1,128)S(1)}, u32[]{:S(2)}, u32[]{:S(2)}) %all-to-all-start.4) | async-done | bytes 160 | tf_op jit(solution)/shard_map/all_to_all | solution.py:18
  77.8 3.4 %multiply_reduce_fusion.1 = (f32[4096]{0:T(1024)S(1)}, f32[4096]{0:T(1024)S(1)}, f32[256,4096]{1,0:T(8,128)S(1)}) fusion(f32[256,4096]{1,0:T(8,128)} %get-tuple-element.13, f32[]{:T(128)S(6)} %mul.75, f32[256]{0:T(256)S(1)} %convert_element_type.10, s32[256]{0:T(256)S(1)} %copy-done.6, s32[4096]{0:T(1024)S(1)} %add_select_fusion), kind=kLoop, calls=%fused_computation.21 | loop fusion | flops 9428992 | bytes 8439812 | tf_op jit(solution)/shard_map/reduce_sum | solution.py:125
  81.3 2.2 fusion.10
  83.8 5.9 %all_to_all.105 = f32[2,32,1152]{2,1,0:T(8,128)S(1)} all-to-all(f32[2,32,1152]{2,1,0:T(8,128)S(1)} %bitcast.89), channel_id=1, replica_groups=mesh['tiles_0'=8,'tiles_1'=4,'tiles_2'=2,'pix'=8] {'tiles_2'}, dimensions={0} | all-to-all | bytes 589824 | tf_op jit(solution)/shard_map/all_to_all | solution.py:58
  89.7 4.4 %all-to-all-start.2 = ((f32[64,1,256]{2,1,0:T(1,128)}), f32[64,1,256]{2,1,0:T(1,128)S(1)}, u32[]{:S(2)}, u32[]{:S(2)}) async-start(f32[64,1,256]{2,1,0:T(1,128)} %reshape.95), calls=%async_computation.2 | async-start | bytes 131072 | tf_op jit(solution)/shard_map/all_to_all | solution.py:18
  94.1 0.8 all_to_all.72
  94.8 9.3 %all-to-all-done.2 = f32[64,1,256]{2,1,0:T(1,128)S(1)} async-done(((f32[64,1,256]{2,1,0:T(1,128)}), f32[64,1,256]{2,1,0:T(1,128)S(1)}, u32[]{:S(2)}, u32[]{:S(2)}) %all-to-all-start.2) | async-done | bytes 65568 | tf_op jit(solution)/shard_map/all_to_all | solution.py:18
  104.2 4.0 %all-to-all-start.6 = ((f32[32,1,1152]{2,1,0:T(1,128)}), f32[32,1,1152]{2,1,0:T(1,128)S(1)}, u32[]{:S(2)}, u32[]{:S(2)}) async-start(f32[32,1,1152]{2,1,0:T(1,128)} %all_to_all.72), calls=%async_computation.6 | async-start | bytes 294912 | tf_op jit(solution)/shard_map/all_to_all | solution.py:66
  108.2 0.7 reduce.11
  109.4 1.5 cholesky.85
  110.9 7.4 %all-to-all-done.6 = f32[32,1,1152]{2,1,0:T(1,128)S(1)} async-done(((f32[32,1,1152]{2,1,0:T(1,128)}), f32[32,1,1152]{2,1,0:T(1,128)S(1)}, u32[]{:S(2)}, u32[]{:S(2)}) %all-to-all-start.6) | async-done | bytes 147488 | tf_op jit(solution)/shard_map/all_to_all | solution.py:66
  118.3 0.7 broadcast_in_dim.48
  119.1 3.9 %all-to-all-start.7 = ((f32[32,1,1152]{2,1,0:T(1,128)}), f32[32,1,1152]{2,1,0:T(1,128)S(1)}, u32[]{:S(2)}, u32[]{:S(2)}) async-start(f32[32,1,1152]{2,1,0:T(1,128)} %broadcast_in_dim.48), calls=%async_computation.7 | async-start | bytes 294912 | tf_op jit(solution)/shard_map/all_to_all | solution.py:18
  124.2 1.2 custom-call.15
  125.5 7.0 %all-to-all-done.7 = f32[32,1,1152]{2,1,0:T(1,128)S(1)} async-done(((f32[32,1,1152]{2,1,0:T(1,128)}), f32[32,1,1152]{2,1,0:T(1,128)S(1)}, u32[]{:S(2)}, u32[]{:S(2)}) %all-to-all-start.7) | async-done | bytes 147488 | tf_op jit(solution)/shard_map/all_to_all | solution.py:18
  132.5 6.5 %all_to_all.106 = f32[2,32,1152]{2,1,0:T(8,128)S(1)} all-to-all(f32[2,32,1152]{2,1,0:T(8,128)S(1)} %broadcast_in_dim.50), channel_id=1, replica_groups=mesh['tiles_0'=8,'tiles_1'=4,'tiles_2'=2,'pix'=8] {'tiles_2'}, dimensions={0} | all-to-all | bytes 589824 | tf_op jit(solution)/shard_map/all_to_all | solution.py:18
  140.9 0.7 reshape.97
  141.6 3.3 %all-to-all-start.9 = ((f32[8,1,256]{2,1,0:T(1,128)}), f32[8,1,256]{2,1,0:T(1,128)S(1)}, u32[]{:S(2)}, u32[]{:S(2)}) async-start(f32[8,1,256]{2,1,0:T(1,128)} %reshape.97), calls=%async_computation.9 | async-start | bytes 16384 | tf_op jit(solution)/shard_map/all_to_all | solution.py:18
  144.9 3.4 %fusion.3 = f32[256,16]{0,1:T(8,128)S(1)} fusion(f32[16,4096]{1,0:T(8,128)S(1)} %convolution_add_fusion.1, bf16[256,4096]{1,0:T(8,128)(2,1)S(1)} %copy-done.2, f32[4096]{0:T(1024)S(1)} %add.82), kind=kOutput, calls=%fused_computation.11 | convolution fusion | flops 203423744 | bytes 2392064 | tf_op jit(solution)/shard_map/dot_general | solution.py:105
  148.3 3.1 %all-to-all-done.9 = f32[8,1,256]{2,1,0:T(1,128)S(1)} async-done(((f32[8,1,256]{2,1,0:T(1,128)}), f32[8,1,256]{2,1,0:T(1,128)S(1)}, u32[]{:S(2)}, u32[]{:S(2)}) %all-to-all-start.9) | async-done | bytes 8224 | tf_op jit(solution)/shard_map/all_to_all | solution.py:18
  151.4 0.7 broadcast_in_dim.52
  152.1 3.4 %all-to-all-start.10 = ((f32[8,256,16]{1,2,0:T(8,128)}), f32[8,256,16]{1,2,0:T(8,128)S(1)}, u32[]{:S(2)}, u32[]{:S(2)}) async-start(f32[8,256,16]{1,2,0:T(8,128)} %broadcast_in_dim.52), calls=%async_computation.10 | async-start | bytes 262144 | tf_op jit(solution)/shard_map/all_to_all | solution.py:18
  156.4 1.5 cholesky.96
  159.2 1.2 custom-call.16
  160.4 3.2 %all-to-all-done.10 = f32[8,256,16]{1,2,0:T(8,128)S(1)} async-done(((f32[8,256,16]{1,2,0:T(8,128)}), f32[8,256,16]{1,2,0:T(8,128)S(1)}, u32[]{:S(2)}, u32[]{:S(2)}) %all-to-all-start.10) | async-done | bytes 131104 | tf_op jit(solution)/shard_map/all_to_all | solution.py:18
  163.9 6.6 %fusion.4 = (f32[]{:T(128)}, f32[256,4096]{1,0:T(8,128)}) fusion(f32[256]{0:T(256)S(1)} %convert_element_type.10, s32[4096]{0:T(1024)S(1)} %add_select_fusion, s32[256]{0:T(256)S(1)} %copy-done.6, f32[16,256]{1,0:T(8,128)S(1)} %fusion.41, f32[16,4096]{1,0:T(8,128)S(1)} %convolution_add_fusion.1, f32[4096]{0:T(1024)S(1)} %add.82, ...), kind=kOutput, calls=%fused_computation.14 | convolution fusion | flops 209715200 | bytes 6604804 | tf_op jit(solution)/shard_map/dot_general | solution.py:112
  171.1 12.2 %all_to_all.107 = f32[16,1,1]{2,1,0:T(1,128)S(1)} all-to-all(f32[16,1,1]{2,1,0:T(1,128)S(1)} %broadcast_in_dim.54), channel_id=1, replica_groups=mesh['tiles_0'=8,'tiles_1'=4,'tiles_2'=2,'pix'=8] {'tiles_2','pix'}, dimensions={0} | all-to-all | bytes 128 | tf_op jit(solution)/shard_map/all_to_all | solution.py:18
  184.0 1.3 broadcast_in_dim.55
  185.3 4.1 %all-to-all-start.13 = ((f32[32,1,1]{2,1,0:T(1,128)}), f32[32,1,1]{2,1,0:T(1,128)S(1)}, u32[]{:S(2)}, u32[]{:S(2)}) async-start(f32[32,1,1]{2,1,0:T(1,128)} %broadcast_in_dim.55), calls=%async_computation.13 | async-start | bytes 32768 | tf_op jit(solution)/shard_map/all_to_all | solution.py:18
  189.5 0.9 reshape.99
  190.4 7.3 %all-to-all-done.13 = f32[32,1,1]{2,1,0:T(1,128)S(1)} async-done(((f32[32,1,1]{2,1,0:T(1,128)}), f32[32,1,1]{2,1,0:T(1,128)S(1)}, u32[]{:S(2)}, u32[]{:S(2)}) %all-to-all-start.13) | async-done | bytes 160 | tf_op jit(solution)/shard_map/all_to_all | solution.py:18
  199.0 3.4 %multiply_reduce_fusion = (f32[4096]{0:T(1024)S(1)}, f32[4096]{0:T(1024)S(1)}, f32[256,4096]{1,0:T(8,128)S(1)}) fusion(f32[256,4096]{1,0:T(8,128)} %get-tuple-element.15, f32[]{:T(128)S(6)} %mul.82, f32[256]{0:T(256)S(1)} %convert_element_type.10, s32[256]{0:T(256)S(1)} %copy-done.6, s32[4096]{0:T(1024)S(1)} %add_select_fusion), kind=kLoop, calls=%fused_computation.18 | loop fusion | flops 9428992 | bytes 8439812 | tf_op jit(solution)/shard_map/reduce_sum | solution.py:125
  202.4 2.2 fusion.8
  204.9 5.4 %all_to_all.108 = f32[2,32,1152]{2,1,0:T(8,128)S(1)} all-to-all(f32[2,32,1152]{2,1,0:T(8,128)S(1)} %bitcast.91), channel_id=1, replica_groups=mesh['tiles_0'=8,'tiles_1'=4,'tiles_2'=2,'pix'=8] {'tiles_2'}, dimensions={0} | all-to-all | bytes 589824 | tf_op jit(solution)/shard_map/all_to_all | solution.py:58
  210.3 4.4 %all-to-all-start.11 = ((f32[64,1,256]{2,1,0:T(1,128)}), f32[64,1,256]{2,1,0:T(1,128)S(1)}, u32[]{:S(2)}, u32[]{:S(2)}) async-start(f32[64,1,256]{2,1,0:T(1,128)} %reshape.99), calls=%async_computation.11 | async-start | bytes 131072 | tf_op jit(solution)/shard_map/all_to_all | solution.py:18
  214.7 0.8 all_to_all.82
  215.5 9.3 %all-to-all-done.11 = f32[64,1,256]{2,1,0:T(1,128)S(1)} async-done(((f32[64,1,256]{2,1,0:T(1,128)}), f32[64,1,256]{2,1,0:T(1,128)S(1)}, u32[]{:S(2)}, u32[]{:S(2)}) %all-to-all-start.11) | async-done | bytes 65568 | tf_op jit(solution)/shard_map/all_to_all | solution.py:18
  224.8 3.9 %all-to-all-start.15 = ((f32[32,1,1152]{2,1,0:T(1,128)}), f32[32,1,1152]{2,1,0:T(1,128)S(1)}, u32[]{:S(2)}, u32[]{:S(2)}) async-start(f32[32,1,1152]{2,1,0:T(1,128)} %all_to_all.82), calls=%async_computation.15 | async-start | bytes 294912 | tf_op jit(solution)/shard_map/all_to_all | solution.py:66
  228.7 0.7 reduce.13
  229.9 1.5 cholesky.107
  231.3 7.4 %all-to-all-done.15 = f32[32,1,1152]{2,1,0:T(1,128)S(1)} async-done(((f32[32,1,1152]{2,1,0:T(1,128)}), f32[32,1,1152]{2,1,0:T(1,128)S(1)}, u32[]{:S(2)}, u32[]{:S(2)}) %all-to-all-start.15) | async-done | bytes 147488 | tf_op jit(solution)/shard_map/all_to_all | solution.py:66
  238.8 0.7 broadcast_in_dim.58
  239.6 3.9 %all-to-all-start.16 = ((f32[32,1,1152]{2,1,0:T(1,128)}), f32[32,1,1152]{2,1,0:T(1,128)S(1)}, u32[]{:S(2)}, u32[]{:S(2)}) async-start(f32[32,1,1152]{2,1,0:T(1,128)} %broadcast_in_dim.58), calls=%async_computation.16 | async-start | bytes 294912 | tf_op jit(solution)/shard_map/all_to_all | solution.py:18
  244.7 1.2 custom-call.17
  245.9 7.0 %all-to-all-done.16 = f32[32,1,1152]{2,1,0:T(1,128)S(1)} async-done(((f32[32,1,1152]{2,1,0:T(1,128)}), f32[32,1,1152]{2,1,0:T(1,128)S(1)}, u32[]{:S(2)}, u32[]{:S(2)}) %all-to-all-start.16) | async-done | bytes 147488 | tf_op jit(solution)/shard_map/all_to_all | solution.py:18
  253.0 6.5 %all_to_all.109 = f32[2,32,1152]{2,1,0:T(8,128)S(1)} all-to-all(f32[2,32,1152]{2,1,0:T(8,128)S(1)} %broadcast_in_dim.60), channel_id=1, replica_groups=mesh['tiles_0'=8,'tiles_1'=4,'tiles_2'=2,'pix'=8] {'tiles_2'}, dimensions={0} | all-to-all | bytes 589824 | tf_op jit(solution)/shard_map/all_to_all | solution.py:18
  260.5 1.1 convolution_add_fusion
  (97 shorter events, 16.8 us)
Async XLA Ops:
  2.8 17.4 %all-to-all-start = ((f32[8,1,256]{2,1,0:T(1,128)}), f32[8,1,256]{2,1,0:T(1,128)S(1)}, u32[]{:S(2)}, u32[]{:S(2)}) async-start(f32[8,1,256]{2,1,0:T(1,128)} %reshape.93), calls=%async_computation | async-start | bytes 16384 | tf_op jit(solution)/shard_map/all_to_all | solution.py:18
  20.9 13.7 %all-to-all-start.1 = ((f32[8,256,16]{1,2,0:T(8,128)}), f32[8,256,16]{1,2,0:T(8,128)S(1)}, u32[]{:S(2)}, u32[]{:S(2)}) async-start(f32[8,256,16]{1,2,0:T(8,128)} %broadcast_in_dim.42), calls=%async_computation.1 | async-start | bytes 262144 | tf_op jit(solution)/shard_map/all_to_all | solution.py:18
  35.0 42.8 %copy-start.6 = (s32[256]{0:T(256)S(1)}, s32[256]{0:T(256)}, u32[]{:S(2)}) copy-start(s32[256]{0:T(256)} %param.12) | copy-start | bytes 3076
  58.3 18.2 %all-to-all-start.4 = ((f32[32,1,1]{2,1,0:T(1,128)}), f32[32,1,1]{2,1,0:T(1,128)S(1)}, u32[]{:S(2)}, u32[]{:S(2)}) async-start(f32[32,1,1]{2,1,0:T(1,128)} %broadcast_in_dim.45), calls=%async_computation.4 | async-start | bytes 32768 | tf_op jit(solution)/shard_map/all_to_all | solution.py:18
  77.8 3.5 %copy-start.1 = (f32[256,4096]{1,0:T(8,128)S(1)}, f32[256,4096]{1,0:T(8,128)}, u32[]{:S(2)}) copy-start(f32[256,4096]{1,0:T(8,128)} %get-tuple-element.13) | copy-start | bytes 12582916
  83.5 56.5 %copy-start.3 = (f32[16,4096]{1,0:T(8,128)S(1)}, f32[16,4096]{1,0:T(8,128)}, u32[]{:S(2)}) copy-start(f32[16,4096]{1,0:T(8,128)} %param.13) | copy-start | bytes 786436
  83.8 56.6 %copy-start.5 = (f32[4096]{0:T(1024)S(1)}, f32[4096]{0:T(1024)}, u32[]{:S(2)}) copy-start(f32[4096]{0:T(1024)} %param.14) | copy-start | bytes 49156
  83.8 61.1 %copy-start.2 = (bf16[256,4096]{1,0:T(8,128)(2,1)S(1)}, bf16[256,4096]{1,0:T(8,128)(2,1)}, u32[]{:S(2)}) copy-start(bf16[256,4096]{1,0:T(8,128)(2,1)} %param.10) | copy-start | bytes 6291460
  89.7 14.5 %all-to-all-start.2 = ((f32[64,1,256]{2,1,0:T(1,128)}), f32[64,1,256]{2,1,0:T(1,128)S(1)}, u32[]{:S(2)}, u32[]{:S(2)}) async-start(f32[64,1,256]{2,1,0:T(1,128)} %reshape.95), calls=%async_computation.2 | async-start | bytes 131072 | tf_op jit(solution)/shard_map/all_to_all | solution.py:18
  104.2 14.1 %all-to-all-start.6 = ((f32[32,1,1152]{2,1,0:T(1,128)}), f32[32,1,1152]{2,1,0:T(1,128)S(1)}, u32[]{:S(2)}, u32[]{:S(2)}) async-start(f32[32,1,1152]{2,1,0:T(1,128)} %all_to_all.72), calls=%async_computation.6 | async-start | bytes 294912 | tf_op jit(solution)/shard_map/all_to_all | solution.py:66
  119.1 13.4 %all-to-all-start.7 = ((f32[32,1,1152]{2,1,0:T(1,128)}), f32[32,1,1152]{2,1,0:T(1,128)S(1)}, u32[]{:S(2)}, u32[]{:S(2)}) async-start(f32[32,1,1152]{2,1,0:T(1,128)} %broadcast_in_dim.48), calls=%async_computation.7 | async-start | bytes 294912 | tf_op jit(solution)/shard_map/all_to_all | solution.py:18
  141.6 9.9 %all-to-all-start.9 = ((f32[8,1,256]{2,1,0:T(1,128)}), f32[8,1,256]{2,1,0:T(1,128)S(1)}, u32[]{:S(2)}, u32[]{:S(2)}) async-start(f32[8,1,256]{2,1,0:T(1,128)} %reshape.97), calls=%async_computation.9 | async-start | bytes 16384 | tf_op jit(solution)/shard_map/all_to_all | solution.py:18
  152.1 11.5 %all-to-all-start.10 = ((f32[8,256,16]{1,2,0:T(8,128)}), f32[8,256,16]{1,2,0:T(8,128)S(1)}, u32[]{:S(2)}, u32[]{:S(2)}) async-start(f32[8,256,16]{1,2,0:T(8,128)} %broadcast_in_dim.52), calls=%async_computation.10 | async-start | bytes 262144 | tf_op jit(solution)/shard_map/all_to_all | solution.py:18
  163.9 38.4 %copy-start.4 = (f32[16,256]{1,0:T(8,128)}, f32[16,256]{1,0:T(8,128)S(1)}, u32[]{:S(2)}) copy-start(f32[16,256]{1,0:T(8,128)S(1)} %fusion.41) | copy-start | bytes 49156
  185.3 12.4 %all-to-all-start.13 = ((f32[32,1,1]{2,1,0:T(1,128)}), f32[32,1,1]{2,1,0:T(1,128)S(1)}, u32[]{:S(2)}, u32[]{:S(2)}) async-start(f32[32,1,1]{2,1,0:T(1,128)} %broadcast_in_dim.55), calls=%async_computation.13 | async-start | bytes 32768 | tf_op jit(solution)/shard_map/all_to_all | solution.py:18
  198.9 3.5 %copy-start = (f32[256,4096]{1,0:T(8,128)S(1)}, f32[256,4096]{1,0:T(8,128)}, u32[]{:S(2)}) copy-start(f32[256,4096]{1,0:T(8,128)} %get-tuple-element.15) | copy-start | bytes 12582916
  210.3 14.5 %all-to-all-start.11 = ((f32[64,1,256]{2,1,0:T(1,128)}), f32[64,1,256]{2,1,0:T(1,128)S(1)}, u32[]{:S(2)}, u32[]{:S(2)}) async-start(f32[64,1,256]{2,1,0:T(1,128)} %reshape.99), calls=%async_computation.11 | async-start | bytes 131072 | tf_op jit(solution)/shard_map/all_to_all | solution.py:18
  224.8 13.9 %all-to-all-start.15 = ((f32[32,1,1152]{2,1,0:T(1,128)}), f32[32,1,1152]{2,1,0:T(1,128)S(1)}, u32[]{:S(2)}, u32[]{:S(2)}) async-start(f32[32,1,1152]{2,1,0:T(1,128)} %all_to_all.82), calls=%async_computation.15 | async-start | bytes 294912 | tf_op jit(solution)/shard_map/all_to_all | solution.py:66
  239.6 13.4 %all-to-all-start.16 = ((f32[32,1,1152]{2,1,0:T(1,128)}), f32[32,1,1152]{2,1,0:T(1,128)S(1)}, u32[]{:S(2)}, u32[]{:S(2)}) async-start(f32[32,1,1152]{2,1,0:T(1,128)} %broadcast_in_dim.58), calls=%async_computation.16 | async-start | bytes 294912 | tf_op jit(solution)/shard_map/all_to_all | solution.py:18
where the time goes:
time: 263 us; the launch traced here: 262 us
  waiting for transfers between devices  71.9 us (27%)
  starting transfers between devices  61.5 us (23%)
  blocking collectives  49.5 us (19%)
  matrix products  32.2 us (12%)
  other arithmetic  29.9 us (11%)
  local copies, waits for them, and re-layouts  14.5 us (6%)
    all_to_all x10, waiting for transfers between devices, sent_to_all(): lax.all_to_all(jnp.broadcast_to(x[None], (length, *x.shape)), axis, 0, 0,...  57.2 us
    all_to_all x10, starting transfers between devices, sent_to_all(): lax.all_to_all(jnp.broadcast_to(x[None], (length, *x.shape)), axis, 0, 0,...  53.6 us
    all_to_all x4, blocking collectives, sent_to_all(): lax.all_to_all(jnp.broadcast_to(x[None], (length, *x.shape)), axis, 0, 0,...  38.3 us
    all_to_all x2, waiting for transfers between devices, summed_rows(): lax.all_to_all(nearer, far, split_axis=0, concat_axis=0, tiled=True)  14.7 us
    dot_general x2, matrix products, local(): residual = shifted - jnp.dot(coefficients, basis, precision=precise)  14.4 us
    all_to_all x2, blocking collectives, sent_and_summed(): pieces = lax.all_to_all(split_up(x, dim, length), axis, 0, 0, tiled=True)  11.3 us
    another operation x12, other arithmetic, solve_gram(): factor = jnp.linalg.cholesky(gram_matrix)  8.5 us
    dot_general x2, matrix products, local(): local_proj = jnp.dot(shifted, basis.T, precision=precise)  8.34 us
  transfers between devices with their start and end apart: 12, of which 12 were waited for; matrix products, arithmetic and copies ran while one was open for 12% of the time, Pallas kernels for 0%

commit v1 on v0

v1 whole, which is shorter than its diff:
```python
import functools

import jax
import jax.numpy as jnp
from jax import lax
from jax.experimental import pallas as pl
from jax.experimental.pallas import tpu as pltpu
from jax.sharding import Mesh
from jax.sharding import PartitionSpec as P

ROW_PX = 2048
BLOCK = 128
ITERS = 2
TILES = ("tiles_0", "tiles_1", "tiles_2")
MESH = pl.DeviceIdType.MESH
HIGHEST = lax.Precision.HIGHEST
RIDGE = 0.01
F32 = jnp.float32
BF16 = jnp.bfloat16

NT = (((1,), (1,)), ((), ()))
NN = (((1,), (0,)), ((), ()))


def split2(x):
    high = x.astype(BF16)
    low = (x - high.astype(F32)).astype(BF16)
    return high, low


def inverse(a):
    rows = a.shape[0]
    lane = lax.broadcasted_iota(jnp.int32, a.shape, 1)
    sub = lax.broadcasted_iota(jnp.int32, a.shape, 0)
    for k in range(rows):
        scale = 1.0 / a[k : k + 1, k : k + 1]
        row = jnp.where(lane[:1] == k, 1.0, a[k : k + 1, :]) * scale
        col = a[:, k : k + 1]
        a = jnp.where(sub == k, row, jnp.where(lane == k, 0.0, a) - col * row)
    return a


def fit_kernel(
    sizes,
    frames_hbm,
    valid_ref,
    fore_ref,
    basis_ref,
    dark_ref,
    basis_out,
    dark_out,
    coef_out,
    frames,
    resid,
    stack,
    coef_lhs,
    term_lhs,
    limit,
    gram_z,
    proj_z,
    sq_z,
    sq_g,
    sq_y,
    cg_g,
    cg_y,
    part,
    from_core,
    x_src,
    x_in,
    y_src,
    y_in,
    full,
    load_sem,
    s_gram,
    r_gram,
    s_proj,
    r_proj,
    s_sqz,
    r_sqz,
    s_sqg,
    r_sqg,
    s_sqy,
    r_sqy,
    s_cgg,
    r_cgg,
    s_cgy,
    r_cgy,
    s_core,
    r_core,
    s_x,
    r_x,
    s_y,
    r_y,
    s_ya,
    r_ya,
    s_xa,
    r_xa,
    s_ca,
    r_ca,
):
    NY, NX, NC, NZ, T, PX, K = sizes
    NG = NX * NC
    GW = PX // NG
    NB = GW // BLOCK
    y, x, c, z = (lax.axis_index(n) for n in (*TILES, "pix"))
    gi = x * NC + c
    other = 1 - c
    tiles_all = T * NY * NX * NC
    pixels_all = PX * NZ

    def y_dev(yy):
        return {"tiles_0": yy}

    def x_dev(xx):
        return {"tiles_1": xx}

    def g_dev(g):
        return {"tiles_1": g // NC, "tiles_2": g % NC}

    def z_dev(zz):
        return {"pix": zz}

    def c_dev():
        return {"tiles_2": other}

    loads = [
        pltpu.make_async_copy(
            frames_hbm.at[:, pl.ds(g * GW, GW)], frames.at[:, pl.ds(g * GW, GW)], load_sem.at[g]
        )
        for g in range(NG)
    ]
    for load in loads:
        load.start()

    barrier = pltpu.get_barrier_semaphore()
    for size, me, dev in ((NZ, z, z_dev), (NG, gi, g_dev), (NY, y, y_dev)):
        for o in range(1, size):
            pl.semaphore_signal(
                barrier, inc=1, device_id=dev(lax.rem(me + o, size)), device_id_type=MESH
            )

    sent = []

    def copy(src, dst, ssem, rsem, dev):
        return pltpu.make_async_remote_copy(
            src_ref=src,
            dst_ref=dst,
            send_sem=ssem,
            recv_sem=rsem,
            device_id=dev,
            device_id_type=MESH,
        )

    def start(*args):
        made = copy(*args)
        made.start()
        sent.append(made)

    def to_all(buf, ssem, rsem, size, me, dev):
        for o in range(1, size):
            start(buf.at[me], buf.at[me], ssem.at[o], rsem.at[me], dev(lax.rem(me + o, size)))

    def from_all(buf, ssem, rsem, size, me, dev):
        for o in range(1, size):
            src = lax.rem(me + o, size)
            copy(buf.at[src], buf.at[src], ssem.at[o], rsem.at[src], dev(src)).wait_recv()

    def summed(buf, size):
        total = buf[0]
        for i in range(1, size):
            total = total + buf[i]
        return total

    valid_row = valid_ref[...].astype(F32)
    limit_row = jnp.where(valid_ref[...] > 0, fore_ref[...].astype(F32), 1000.0)
    limit[...] = jnp.broadcast_to(limit_row, (BLOCK, T)).T

    def usable(block):
        kind = lax.rem(z * (NG * NB) + block, ROW_PX // BLOCK).astype(F32)
        return limit[...] <= kind

    row16 = lax.broadcasted_iota(jnp.int32, (16, GW), 0)

    def cols_of(g):
        return pl.ds(pl.multiple_of(g * GW, GW), GW)

    def prepare(g, gram):
        cols = cols_of(g)
        high, low = split2(basis_out[:, cols])
        d = dark_out[:, cols]
        d_high = d.astype(BF16).astype(F32)
        d_mid = (d - d_high).astype(BF16).astype(F32)
        d_low = d - d_high - d_mid
        dark_rows = jnp.where(
            row16 == 0,
            d_high,
            jnp.where(row16 == 1, d_mid, jnp.where(row16 == 2, d_low, 0.0)),
        )
        pieces = jnp.concatenate([high, low, high, dark_rows.astype(BF16)], axis=0)
        stack[:, cols] = pieces
        return gram + lax.dot_general(pieces[: 2 * K], pieces, NT, preferred_element_type=F32)

    def project(g, proj):
        cols = cols_of(g)
        return proj + lax.dot_general(
            stack[: 2 * K, cols], frames[:, cols], NT, preferred_element_type=F32
        )

    gram0 = jnp.zeros((2 * K, 4 * K), F32)
    proj0 = jnp.zeros((2 * K, T), F32)

    basis_out[...] = basis_ref[...]
    dark_out[...] = dark_ref[...]
    for it in range(ITERS):
        for buf in (gram_z, cg_g):
            buf[it, pl.ds(z if buf is gram_z else gi, 1)] = jnp.zeros((1, K, BLOCK), F32)
    lane = lax.broadcasted_iota(jnp.int32, (K, BLOCK), 1)
    sub = lax.broadcasted_iota(jnp.int32, (K, BLOCK), 0)
    ridge = jnp.where(lane == sub, RIDGE, 0.0)

    gram = lax.fori_loop(0, NG, prepare, gram0)
    pl.semaphore_wait(barrier, (NZ - 1) + (NG - 1) + (NY - 1))

    for it in range(ITERS):
        last = it == ITERS - 1

        def at(ref):
            return ref.at[it]

        gram_z[it, pl.ds(z, 1), :, : 4 * K] = (gram[:K] + gram[K:])[None]
        to_all(at(gram_z), at(s_gram), at(r_gram), NZ, z, z_dev)
        if it == 0:
            proj = proj0
            for g in range(NG):
                loads[g].wait()
                proj = project(g, proj)
        proj_z[it, pl.ds(z, 1)] = (proj[:K] + proj[K:])[None]
        to_all(at(proj_z), at(s_proj), at(r_proj), NZ, z, z_dev)

        from_all(at(gram_z), at(s_gram), at(r_gram), NZ, z, z_dev)
        raw = summed(at(gram_z), NZ)
        dark_dot = jnp.sum(
            jnp.where((lane >= 3 * K) & (lane < 3 * K + 3), raw, 0.0), axis=1, keepdims=True
        )
        gram_f = jnp.where(lane < K, raw + pltpu.roll(raw, BLOCK - K, 1), 0.0) / pixels_all
        solver = inverse(gram_f + ridge)
        from_all(at(proj_z), at(s_proj), at(r_proj), NZ, z, z_dev)
        right = (summed(at(proj_z), NZ) - dark_dot) / pixels_all
        coef = lax.dot_general(
            solver[:, :K], right, NN, precision=HIGHEST, preferred_element_type=F32
        )
        if last:
            coef_out[...] = coef

        cg = lax.dot_general(
            coef * valid_row, coef, NT, precision=HIGHEST, preferred_element_type=F32
        )
        cg_g[it, pl.ds(gi, 1), :, :K] = cg[None]
        to_all(at(cg_g), at(s_cgg), at(r_cgg), NG, gi, g_dev)

        c_high = coef.astype(BF16).astype(F32)
        c_stack = jnp.concatenate(
            [c_high, c_high, coef - c_high, jnp.ones((K, T), F32)], axis=0
        )
        coef_lhs[...] = c_stack.T.astype(BF16)

        def residual(g, acc):
            cols = cols_of(g)
            fitted = lax.dot_general(
                coef_lhs[...], stack[:, cols], NN, preferred_element_type=F32
            )
            r = frames[:, cols].astype(F32) - fitted
            resid[:, cols] = r
            for j in range(NB):
                rj = r[:, j * BLOCK : (j + 1) * BLOCK]
                sq = jnp.where(usable(g * NB + j), rj * rj, 0.0)
                acc = acc + jnp.sum(sq.reshape(T // 8, 8, BLOCK), axis=0)
            return acc

        acc = lax.fori_loop(0, NG, residual, jnp.zeros((8, BLOCK), F32))
        sq_z[it, pl.ds(z, 1)] = jnp.sum(acc, axis=0, keepdims=True)[None]
        to_all(at(sq_z), at(s_sqz), at(r_sqz), NZ, z, z_dev)

        from_all(at(cg_g), at(s_cgg), at(r_cgg), NG, gi, g_dev)
        cg_y[it, pl.ds(y, 1)] = summed(at(cg_g), NG)[None]
        to_all(at(cg_y), at(s_cgy), at(r_cgy), NY, y, y_dev)

        from_all(at(sq_z), at(s_sqz), at(r_sqz), NZ, z, z_dev)
        sq_g[it, pl.ds(gi, 1)] = summed(at(sq_z), NZ)[None]
        to_all(at(sq_g), at(s_sqg), at(r_sqg), NG, gi, g_dev)
        from_all(at(sq_g), at(s_sqg), at(r_sqg), NG, gi, g_dev)
        sq_y[it, pl.ds(y, 1)] = summed(at(sq_g), NG)[None]
        to_all(at(sq_y), at(s_sqy), at(r_sqy), NY, y, y_dev)

        from_all(at(cg_y), at(s_cgy), at(r_cgy), NY, y, y_dev)
        gram_c = jnp.where(lane < K, summed(at(cg_y), NY) / tiles_all, 0.0)
        solver_c = inverse(gram_c + ridge)
        solved = lax.dot_general(
            solver_c[:, :K], coef, NN, precision=HIGHEST, preferred_element_type=F32
        ) / tiles_all
        high, low = split2(solved)
        term_lhs[...] = jnp.concatenate([high, low], axis=0)

        from_all(at(sq_y), at(s_sqy), at(r_sqy), NY, y, y_dev)
        square = jnp.sum(summed(at(sq_y), NY), axis=1, keepdims=True)
        spread = square / (float(tiles_all) * float(pixels_all)) + 1e-05
        rate = 1.0 / (4.0 * spread)

        def terms(cc, xx):
            g = cc * NX + xx
            for j in range(NB):
                cols = pl.ds(pl.multiple_of(g * GW + j * BLOCK, BLOCK), BLOCK)
                r = resid[:, cols]
                w = jnp.where(usable(g * NB + j), 1.0 / (1.0 + r * r * rate), 0.0)
                wr = w * r
                high, low = split2(wr)
                a = lax.dot_general(term_lhs[...], high, NN, preferred_element_type=F32)
                b = lax.dot_general(term_lhs[:K], low, NN, preferred_element_type=F32)
                tile = a[:K] + a[K:] + b
                part[it, cc, xx, pl.ds(2 * j, 2)] = tile.reshape(2, 8, BLOCK)
                part[it, cc, xx, NY, 2 * j : 2 * j + 1, :] = jnp.sum(wr, axis=0, keepdims=True)
                part[it, cc, xx, NY, 2 * j + 1 : 2 * j + 2, :] = jnp.sum(
                    w, axis=0, keepdims=True
                )

        def core_copy(xx):
            return copy(
                part.at[it, other, xx],
                from_core.at[it, xx],
                s_core.at[it, xx],
                r_core.at[it, xx],
                c_dev(),
            )

        def x_copy(xx):
            return copy(
                x_src.at[it, xx], x_in.at[it, x], s_x.at[it, xx], r_x.at[it, x], x_dev(xx)
            )

        @pl.loop(0, NX)
        def _(i):
            xx = lax.rem(x + 1 + i, NX)
            terms(other, xx)
            core_copy(xx).start()

        @pl.loop(0, NX)
        def _(i):
            xx = lax.rem(x + 1 + i, NX)
            terms(c, xx)
            core_copy(xx).wait_recv()
            both = part[it, c, xx] + from_core[it, xx]

            @pl.when(i < NX - 1)
            def _():
                x_src[it, xx] = both
                x_copy(xx).start()

            @pl.when(i == NX - 1)
            def _():
                x_in[it, x] = both

        for o in range(1, NX):
            src = lax.rem(x + o, NX)
            copy(
                x_src.at[it, src], x_in.at[it, src], s_x.at[it, src], r_x.at[it, src], x_dev(src)
            ).wait_recv()
        mine = summed(at(x_in), NX)
        for i in range(NY):
            y_src[it, i, 0] = mine[i]
            y_src[it, i, 1] = mine[NY]
        y_in[it, y] = y_src[it, y]
        for o in range(1, NY):
            yy = lax.rem(y + o, NY)
            start(y_src.at[it, yy], y_in.at[it, y], s_y.at[it, o], r_y.at[it, y], y_dev(yy))
        for o in range(1, NY):
            src = lax.rem(y + o, NY)
            copy(
                y_src.at[it, src], y_in.at[it, src], s_y.at[it, o], r_y.at[it, src], y_dev(src)
            ).wait_recv()
        done = summed(at(y_in), NY)
        full[it, c, x, y] = done[0]
        full[it, c, x, NY] = done[1]

        for o in range(1, NY):
            yy = lax.rem(y + o, NY)
            start(
                full.at[it, c, x, y],
                full.at[it, c, x, y],
                s_ya.at[it, o],
                r_ya.at[it, y],
                y_dev(yy),
            )
        for o in range(1, NY):
            src = lax.rem(y + o, NY)
            copy(
                full.at[it, c, x, src],
                full.at[it, c, x, src],
                s_ya.at[it, o],
                r_ya.at[it, src],
                y_dev(src),
            ).wait_recv()

        def gather_copy(xx, dev, ssem, rsem):
            return copy(full.at[it, c, xx], full.at[it, c, xx], ssem, rsem, dev)

        for o in range(1, NX):
            xx = lax.rem(x + o, NX)
            start(
                full.at[it, c, x],
                full.at[it, c, x],
                s_xa.at[it, o],
                r_xa.at[it, x],
                x_dev(xx),
            )
        start(full.at[it, c, x], full.at[it, c, x], s_ca.at[it, 0], r_ca.at[it, x], c_dev())
        for o in range(1, NX):
            src = lax.rem(x + o, NX)
            gather_copy(src, x_dev(src), s_xa.at[it, o], r_xa.at[it, src]).wait_recv()
            start(
                full.at[it, c, src],
                full.at[it, c, src],
                s_ca.at[it, o],
                r_ca.at[it, src],
                c_dev(),
            )

        def apply(cc, xx):
            g = cc * NX + xx
            for j in range(NB):
                cols = pl.ds(pl.multiple_of(g * GW + j * BLOCK, BLOCK), BLOCK)
                delta = full[it, cc, xx, pl.ds(2 * j, 2)].reshape(K, BLOCK)
                basis_out[:, cols] = basis_out[:, cols] + delta
                top = full[it, cc, xx, NY, 2 * j : 2 * j + 1, :]
                low = full[it, cc, xx, NY, 2 * j + 1 : 2 * j + 2, :]
                dark_out[:, cols] = dark_out[:, cols] + top / (low + 1.0)
            return g

        def own(i, carry):
            g = apply(c, i)
            if last:
                return carry
            gram, proj = carry
            return prepare(g, gram), project(g, proj)

        def partner(i, carry):
            copy(
                full.at[it, other, i],
                full.at[it, other, i],
                s_ca.at[it, 0],
                r_ca.at[it, i],
                c_dev(),
            ).wait_recv()
            g = apply(other, i)
            if last:
                return carry
            gram, proj = carry
            return prepare(g, gram), project(g, proj)

        carry = 0 if last else (gram0, proj0)
        carry = lax.fori_loop(0, NX, own, carry)
        carry = lax.fori_loop(0, NX, partner, carry)
        if not last:
            gram, proj = carry

        for xx in range(NX):
            core_copy(xx).wait_send()
        for o in range(1, NX):
            x_copy(lax.rem(x + o, NX)).wait_send()

    for made in sent:
        made.wait_send()


def local(frames, tile_valid, foreground_blocks, basis_start, dark_start):
    T, PX = frames.shape
    K = basis_start.shape[0]
    NY, NX, NC, NZ = (lax.axis_size(n) for n in (*TILES, "pix"))
    NG = NX * NC
    vmem = pl.BlockSpec(memory_space=pltpu.VMEM)
    dma = pltpu.SemaphoreType.DMA
    scratch = [
        pltpu.VMEM((T, PX), BF16),
        pltpu.VMEM((T, PX), F32),
        pltpu.VMEM((4 * K, PX), BF16),
        pltpu.VMEM((T, 4 * K), BF16),
        pltpu.VMEM((2 * K, T), BF16),
        pltpu.VMEM((T, BLOCK), F32),
        pltpu.VMEM((ITERS, NZ, K, BLOCK), F32),
        pltpu.VMEM((ITERS, NZ, K, T), F32),
        pltpu.VMEM((ITERS, NZ, 1, BLOCK), F32),
        pltpu.VMEM((ITERS, NG, 1, BLOCK), F32),
        pltpu.VMEM((ITERS, NY, 1, BLOCK), F32),
        pltpu.VMEM((ITERS, NG, K, BLOCK), F32),
        pltpu.VMEM((ITERS, NY, K, BLOCK), F32),
        pltpu.VMEM((ITERS, NC, NX, NY + 1, 8, BLOCK), F32),
        pltpu.VMEM((ITERS, NX, NY + 1, 8, BLOCK), F32),
        pltpu.VMEM((ITERS, NX, NY + 1, 8, BLOCK), F32),
        pltpu.VMEM((ITERS, NX, NY + 1, 8, BLOCK), F32),
        pltpu.VMEM((ITERS, NY, 2, 8, BLOCK), F32),
        pltpu.VMEM((ITERS, NY, 2, 8, BLOCK), F32),
        pltpu.VMEM((ITERS, NC, NX, NY + 1, 8, BLOCK), F32),
        dma((NG,)),
    ]
    for size in (NZ, NZ, NZ, NG, NY, NG, NY, NX, NX, NY, NY, NX, NX):
        scratch += [dma((ITERS, size)), dma((ITERS, size))]
    basis, dark, coef = pl.pallas_call(
        functools.partial(fit_kernel, (NY, NX, NC, NZ, T, PX, K)),
        out_shape=(
            jax.ShapeDtypeStruct((K, PX), F32),
            jax.ShapeDtypeStruct((1, PX), F32),
            jax.ShapeDtypeStruct((K, T), F32),
        ),
        in_specs=[pl.BlockSpec(memory_space=pl.ANY), vmem, vmem, vmem, vmem],
        out_specs=(vmem, vmem, vmem),
        scratch_shapes=scratch,
        compiler_params=pltpu.CompilerParams(
            collective_id=0, has_side_effects=True, vmem_limit_bytes=48 * 1024 * 1024
        ),
    )(
        frames,
        tile_valid.reshape(1, T),
        foreground_blocks.reshape(1, T),
        basis_start,
        dark_start.reshape(1, PX),
    )
    return basis, dark.reshape(PX), coef.T


def solution(mesh):
    finer = Mesh(
        mesh.devices.reshape(8, 4, 2, mesh.shape["pix"]), ("tiles_0", "tiles_1", "tiles_2", "pix")
    )
    in_specs = (P(TILES, "pix"), P(TILES), P(TILES), P(None, "pix"), P("pix"))
    out_specs = (P(None, "pix"), P("pix"), P(TILES, None))
    return jax.shard_map(local, mesh=finer, in_specs=in_specs, out_specs=out_specs, check_vma=False)
```

time: 263 us -> 114 us (0.43)
  Pallas kernels: 0 us -> 107 us
  waiting for transfers between devices: 71.9 us -> 0 us
  starting transfers between devices: 61.5 us -> 0 us
  blocking collectives: 49.5 us -> 0 us
  matrix products: 32.2 us -> 0 us
  other arithmetic: 29.9 us -> 0 us
  local copies, waits for them, and re-layouts: 14.5 us -> 6.52 us
    pallas_call x0 -> x1, Pallas kernels: none -> 107 us  [local(): pl.pallas_call(functools.partial(fit_kernel, (NY, NX, NC, NZ, T, PX, K)),...]
    all_to_all x12 -> x0, waiting for transfers between devices: 71.9 us -> none  [the longest x10 57.2 us: sent_to_all(): lax.all_to_all(jnp.broadcast_to(x[None], (length, *x.shape)), axis, 0, 0,...]
    all_to_all x12 -> x0, starting transfers between devices: 61.5 us -> none  [the longest x10 53.6 us: sent_to_all(): lax.all_to_all(jnp.broadcast_to(x[None], (length, *x.shape)), axis, 0, 0,...]
    all_to_all x6 -> x0, blocking collectives: 49.6 us -> none  [the longest x4 38.3 us: sent_to_all(): lax.all_to_all(jnp.broadcast_to(x[None], (length, *x.shape)), axis, 0, 0,...]
    dot_general x10 -> x0, matrix products: 29.3 us -> none  [the longest x2 14.4 us: local(): residual = shifted - jnp.dot(coefficients, basis, precision=precise)]
    another operation x20 -> x0, other arithmetic: 16 us -> none  [the longest x12 8.5 us: solve_gram(): factor = jnp.linalg.cholesky(gram_matrix)]
    reduce_sum x16 -> x0, other arithmetic: 9.76 us -> none  [the longest x2 6.79 us: local(): jnp.sum(weighted, axis=0, keepdims=True)]
    broadcast_in_dim x14 -> x0, local copies, waits for them, and re-layouts: 6.8 us -> none  [sent_to_all(): jnp.broadcast_to(x[None], (length, *x.shape))]
  transfers between devices with their start and end apart: 12 -> 0, of which waited for: 12 -> 0; matrix products, arithmetic and copies ran while one was open for 12% -> 0% of each run, Pallas kernels for 0% -> 0%
where the time goes in v1:
time: 114 us
  Pallas kernels  107 us (94%)
  local copies, waits for them, and re-layouts  6.52 us (6%)
    pallas_call x1, Pallas kernels, local(): pl.pallas_call(functools.partial(fit_kernel, (NY, NX, NC, NZ, T, PX, K)),...  107 us
    unnamed x13, local copies, waits for them, and re-layouts  6.52 us

profile of v1, /device:TPU:1, one launch (start us, length us, event | category | flops | bytes accessed | tf_op | source)
XLA Modules:
  0.0 113.7 jit_solution(3778761644114575331)
XLA Ops:
  0.6 0.0 copy-start
  0.6 1.6 %copy-done = bf16[256,4096]{1,0:T(8,128)(2,1)S(1)} copy-done((bf16[256,4096]{1,0:T(8,128)(2,1)S(1)}, bf16[256,4096]{1,0:T(8,128)(2,1)}, u32[]{:S(2)}) %copy-start) | copy-done | bytes 2097176
  2.2 0.0 copy-start.1
  2.2 0.9 copy-done.1
  3.2 0.0 copy-start.2
  3.2 0.7 copy-done.2
  3.9 0.0 copy-start.3
  3.9 0.7 copy-done.3
  4.6 0.0 copy-start.4
  4.6 0.7 copy-done.4
  5.3 106.6 %shard_map.76 = (f32[16,4096]{1,0:T(8,128)S(1)}, f32[1,4096]{1,0:T(1,128)S(1)}, f32[16,256]{1,0:T(8,128)S(1)}) custom-call(bf16[256,4096]{1,0:T(8,128)(2,1)S(1)} %copy-done, s32[1,256]{1,0:T(1,128)S(1)} %bitcast.8, s32[1,256]{1,0:T(1,128)S(1)} %bitcast.9, f32[16,4096]{1,0:T(8,128)S(1)} %copy-done.1, f32[1,4096]{1,0:T(1,128)S(1)} %bitcast.5), custom_call_target="tpu_custom_call" | custom-call | tf_op jit(solution)/shard_map/pallas_call | solution.py:506
  111.8 0.7 copy.11
  112.5 0.6 copy.12
  113.1 0.6 copy.13
Async XLA Ops:
  0.6 1.6 %copy-start = (bf16[256,4096]{1,0:T(8,128)(2,1)S(1)}, bf16[256,4096]{1,0:T(8,128)(2,1)}, u32[]{:S(2)}) copy-start(bf16[256,4096]{1,0:T(8,128)(2,1)} %frames_hbm.1) | copy-start | bytes 6291460
  2.2 0.9 copy-start.1
  3.2 0.7 copy-start.2
  3.9 0.7 copy-start.3
  4.6 0.7 copy-start.4

commit v2 on v1

--- a/solution.py
+++ b/solution.py
@@ -43,19 +43,23 @@
 def fit_kernel(
     sizes,
     frames_hbm,
-    valid_ref,
-    fore_ref,
-    basis_ref,
-    dark_ref,
+    valid_hbm,
+    fore_hbm,
+    basis_hbm,
+    dark_hbm,
     basis_out,
     dark_out,
     coef_out,
     frames,
+    valid_ref,
+    fore_ref,
     resid,
     stack,
     coef_lhs,
     term_lhs,
     limit,
+    masked,
+    fold,
     gram_z,
     proj_z,
     sq_z,
@@ -69,8 +73,10 @@
     x_in,
     y_src,
     y_in,
+    sum_in,
     full,
     load_sem,
+    small_sem,
     s_gram,
     r_gram,
     s_proj,
@@ -91,6 +97,8 @@
     r_x,
     s_y,
     r_y,
+    s_t,
+    r_t,
     s_ya,
     r_ya,
     s_xa,
@@ -129,7 +137,18 @@
         )
         for g in range(NG)
     ]
-    for load in loads:
+    small = [
+        pltpu.make_async_copy(src, dst, small_sem.at[i])
+        for i, (src, dst) in enumerate(
+            (
+                (valid_hbm, valid_ref),
+                (fore_hbm, fore_ref),
+                (dark_hbm, dark_out),
+                (basis_hbm, basis_out),
+            )
+        )
+    ]
+    for load in small + loads:
         load.start()
 
     barrier = pltpu.get_barrier_semaphore()
@@ -171,13 +190,20 @@
             total = total + buf[i]
         return total
 
+    small[0].wait()
+    small[1].wait()
     valid_row = valid_ref[...].astype(F32)
     limit_row = jnp.where(valid_ref[...] > 0, fore_ref[...].astype(F32), 1000.0)
     limit[...] = jnp.broadcast_to(limit_row, (BLOCK, T)).T
 
-    def usable(block):
-        kind = lax.rem(z * (NG * NB) + block, ROW_PX // BLOCK).astype(F32)
-        return limit[...] <= kind
+    kinds = ROW_PX // BLOCK
+    for k in range(kinds):
+        masked[k : k + 1, :] = jnp.sum(
+            jnp.where(limit[...] > float(k), 1.0, 0.0), axis=0, keepdims=True
+        )
+
+    def kind_of(block):
+        return lax.rem(z * (NG * NB) + block, kinds)
 
     row16 = lax.broadcasted_iota(jnp.int32, (16, GW), 0)
 
@@ -209,15 +235,15 @@
     gram0 = jnp.zeros((2 * K, 4 * K), F32)
     proj0 = jnp.zeros((2 * K, T), F32)
 
-    basis_out[...] = basis_ref[...]
-    dark_out[...] = dark_ref[...]
     for it in range(ITERS):
-        for buf in (gram_z, cg_g):
-            buf[it, pl.ds(z if buf is gram_z else gi, 1)] = jnp.zeros((1, K, BLOCK), F32)
+        cg_g[it, pl.ds(gi, 1)] = jnp.zeros((1, K, BLOCK), F32)
+    fold[...] = jnp.zeros((K, BLOCK), F32)
     lane = lax.broadcasted_iota(jnp.int32, (K, BLOCK), 1)
     sub = lax.broadcasted_iota(jnp.int32, (K, BLOCK), 0)
     ridge = jnp.where(lane == sub, RIDGE, 0.0)
 
+    small[2].wait()
+    small[3].wait()
     gram = lax.fori_loop(0, NG, prepare, gram0)
     pl.semaphore_wait(barrier, (NZ - 1) + (NG - 1) + (NY - 1))
 
@@ -227,7 +253,8 @@
         def at(ref):
             return ref.at[it]
 
-        gram_z[it, pl.ds(z, 1), :, : 4 * K] = (gram[:K] + gram[K:])[None]
+        fold[:, : 4 * K] = gram[:K] + gram[K:]
+        gram_z[it, z] = fold[:8] + pltpu.roll(fold[8:], BLOCK // 2, 1)
         to_all(at(gram_z), at(s_gram), at(r_gram), NZ, z, z_dev)
         if it == 0:
             proj = proj0
@@ -238,7 +265,8 @@
         to_all(at(proj_z), at(s_proj), at(r_proj), NZ, z, z_dev)
 
         from_all(at(gram_z), at(s_gram), at(r_gram), NZ, z, z_dev)
-        raw = summed(at(gram_z), NZ)
+        folded = summed(at(gram_z), NZ)
+        raw = jnp.concatenate([folded, pltpu.roll(folded, BLOCK // 2, 1)], axis=0)
         dark_dot = jnp.sum(
             jnp.where((lane >= 3 * K) & (lane < 3 * K + 3), raw, 0.0), axis=1, keepdims=True
         )
@@ -270,11 +298,11 @@
                 coef_lhs[...], stack[:, cols], NN, preferred_element_type=F32
             )
             r = frames[:, cols].astype(F32) - fitted
-            resid[:, cols] = r
             for j in range(NB):
-                rj = r[:, j * BLOCK : (j + 1) * BLOCK]
-                sq = jnp.where(usable(g * NB + j), rj * rj, 0.0)
-                acc = acc + jnp.sum(sq.reshape(T // 8, 8, BLOCK), axis=0)
+                kind = kind_of(g * NB + j).astype(F32)
+                rj = jnp.where(limit[...] <= kind, r[:, j * BLOCK : (j + 1) * BLOCK], 0.0)
+                resid[:, pl.ds(pl.multiple_of(g * GW + j * BLOCK, BLOCK), BLOCK)] = rj
+                acc = acc + jnp.sum((rj * rj).reshape(T // 8, 8, BLOCK), axis=0)
             return acc
 
         acc = lax.fori_loop(0, NG, residual, jnp.zeros((8, BLOCK), F32))
@@ -311,16 +339,15 @@
             for j in range(NB):
                 cols = pl.ds(pl.multiple_of(g * GW + j * BLOCK, BLOCK), BLOCK)
                 r = resid[:, cols]
-                w = jnp.where(usable(g * NB + j), 1.0 / (1.0 + r * r * rate), 0.0)
+                w = 1.0 / (1.0 + r * r * rate)
                 wr = w * r
-                high, low = split2(wr)
-                a = lax.dot_general(term_lhs[...], high, NN, preferred_element_type=F32)
-                b = lax.dot_general(term_lhs[:K], low, NN, preferred_element_type=F32)
-                tile = a[:K] + a[K:] + b
-                part[it, cc, xx, pl.ds(2 * j, 2)] = tile.reshape(2, 8, BLOCK)
+                a = lax.dot_general(
+                    term_lhs[...], wr.astype(BF16), NN, preferred_element_type=F32
+                )
+                part[it, cc, xx, pl.ds(2 * j, 2)] = (a[:K] + a[K:]).reshape(2, 8, BLOCK)
                 part[it, cc, xx, NY, 2 * j : 2 * j + 1, :] = jnp.sum(wr, axis=0, keepdims=True)
-                part[it, cc, xx, NY, 2 * j + 1 : 2 * j + 2, :] = jnp.sum(
-                    w, axis=0, keepdims=True
+                part[it, cc, xx, NY, 2 * j + 1 : 2 * j + 2, :] = (
+                    jnp.sum(w, axis=0, keepdims=True) - masked[pl.ds(kind_of(g * NB + j), 1), :]
                 )
 
         def core_copy(xx):
@@ -365,64 +392,60 @@
                 x_src.at[it, src], x_in.at[it, src], s_x.at[it, src], r_x.at[it, src], x_dev(src)
             ).wait_recv()
         mine = summed(at(x_in), NX)
-        for i in range(NY):
-            y_src[it, i, 0] = mine[i]
-            y_src[it, i, 1] = mine[NY]
+        near_y = sorted(range(1, NY), key=lambda o: min(o, NY - o))
+        near_x = sorted(range(1, NX), key=lambda o: min(o, NX - o))
+        y_src[it] = mine[:NY]
+        sum_in[it, y] = mine[NY]
         y_in[it, y] = y_src[it, y]
-        for o in range(1, NY):
+        for o in reversed(near_y):
             yy = lax.rem(y + o, NY)
             start(y_src.at[it, yy], y_in.at[it, y], s_y.at[it, o], r_y.at[it, y], y_dev(yy))
-        for o in range(1, NY):
+        to_all(at(sum_in), at(s_t), at(r_t), NY, y, y_dev)
+        for o in near_y:
             src = lax.rem(y + o, NY)
             copy(
                 y_src.at[it, src], y_in.at[it, src], s_y.at[it, o], r_y.at[it, src], y_dev(src)
             ).wait_recv()
-        done = summed(at(y_in), NY)
-        full[it, c, x, y] = done[0]
-        full[it, c, x, NY] = done[1]
-
-        for o in range(1, NY):
-            yy = lax.rem(y + o, NY)
-            start(
-                full.at[it, c, x, y],
-                full.at[it, c, x, y],
-                s_ya.at[it, o],
-                r_ya.at[it, y],
-                y_dev(yy),
-            )
-        for o in range(1, NY):
+        full[it, c, x, y] = summed(at(y_in), NY)
+
+        def tile_copy(xx, tile, dev, ssem, rsem):
+            where = full.at[it, c, xx, tile]
+            return copy(where, where, ssem, rsem, dev)
+
+        def begin(made):
+            made.start()
+            sent.append(made)
+
+        def onward(tile):
+            for o in reversed(near_x):
+                begin(
+                    tile_copy(
+                        x,
+                        tile,
+                        x_dev(lax.rem(x + o, NX)),
+                        s_xa.at[it, o, tile],
+                        r_xa.at[it, x, tile],
+                    )
+                )
+            to_core(x, tile)
+
+        def to_core(xx, tile):
+            begin(
+                tile_copy(xx, tile, c_dev(), s_ca.at[it, xx, tile], r_ca.at[it, xx, tile])
+            )
+
+        for o in reversed(near_y):
+            begin(
+                tile_copy(x, y, y_dev(lax.rem(y + o, NY)), s_ya.at[it, o], r_ya.at[it, y])
+            )
+        onward(y)
+        from_all(at(sum_in), at(s_t), at(r_t), NY, y, y_dev)
+        full[it, c, x, NY] = summed(at(sum_in), NY)
+        onward(NY)
+        for o in near_y:
             src = lax.rem(y + o, NY)
-            copy(
-                full.at[it, c, x, src],
-                full.at[it, c, x, src],
-                s_ya.at[it, o],
-                r_ya.at[it, src],
-                y_dev(src),
-            ).wait_recv()
-
-        def gather_copy(xx, dev, ssem, rsem):
-            return copy(full.at[it, c, xx], full.at[it, c, xx], ssem, rsem, dev)
-
-        for o in range(1, NX):
-            xx = lax.rem(x + o, NX)
-            start(
-                full.at[it, c, x],
-                full.at[it, c, x],
-                s_xa.at[it, o],
-                r_xa.at[it, x],
-                x_dev(xx),
-            )
-        start(full.at[it, c, x], full.at[it, c, x], s_ca.at[it, 0], r_ca.at[it, x], c_dev())
-        for o in range(1, NX):
-            src = lax.rem(x + o, NX)
-            gather_copy(src, x_dev(src), s_xa.at[it, o], r_xa.at[it, src]).wait_recv()
-            start(
-                full.at[it, c, src],
-                full.at[it, c, src],
-                s_ca.at[it, o],
-                r_ca.at[it, src],
-                c_dev(),
-            )
+            tile_copy(x, src, y_dev(src), s_ya.at[it, o], r_ya.at[it, src]).wait_recv()
+            onward(src)
 
         def apply(cc, xx):
             g = cc * NX + xx
@@ -435,29 +458,36 @@
                 dark_out[:, cols] = dark_out[:, cols] + top / (low + 1.0)
             return g
 
-        def own(i, carry):
-            g = apply(c, i)
+        def take(cc, xx, carry):
+            g = apply(cc, xx)
             if last:
                 return carry
             gram, proj = carry
             return prepare(g, gram), project(g, proj)
 
+        carry = 0 if last else (gram0, proj0)
+        carry = take(c, x, carry)
+        for tile in [y, NY] + [lax.rem(y + o, NY) for o in near_y]:
+            for o in near_x:
+                src = lax.rem(x + o, NX)
+                tile_copy(
+                    src, tile, x_dev(src), s_xa.at[it, o, tile], r_xa.at[it, src, tile]
+                ).wait_recv()
+                to_core(src, tile)
+
+        def own(i, carry):
+            return take(c, lax.rem(x + i, NX), carry)
+
         def partner(i, carry):
-            copy(
-                full.at[it, other, i],
-                full.at[it, other, i],
-                s_ca.at[it, 0],
-                r_ca.at[it, i],
-                c_dev(),
-            ).wait_recv()
-            g = apply(other, i)
-            if last:
-                return carry
-            gram, proj = carry
-            return prepare(g, gram), project(g, proj)
-
-        carry = 0 if last else (gram0, proj0)
-        carry = lax.fori_loop(0, NX, own, carry)
+            xx = lax.rem(x + i, NX)
+            for tile in range(NY + 1):
+                where = full.at[it, other, xx, tile]
+                copy(
+                    where, where, s_ca.at[it, xx, tile], r_ca.at[it, xx, tile], c_dev()
+                ).wait_recv()
+            return take(other, xx, carry)
+
+        carry = lax.fori_loop(1, NX, own, carry)
         carry = lax.fori_loop(0, NX, partner, carry)
         if not last:
             gram, proj = carry
@@ -480,12 +510,16 @@
     dma = pltpu.SemaphoreType.DMA
     scratch = [
         pltpu.VMEM((T, PX), BF16),
+        pltpu.VMEM((1, T), jnp.int32),
+        pltpu.VMEM((1, T), jnp.int32),
         pltpu.VMEM((T, PX), F32),
         pltpu.VMEM((4 * K, PX), BF16),
         pltpu.VMEM((T, 4 * K), BF16),
         pltpu.VMEM((2 * K, T), BF16),
         pltpu.VMEM((T, BLOCK), F32),
-        pltpu.VMEM((ITERS, NZ, K, BLOCK), F32),
+        pltpu.VMEM((ROW_PX // BLOCK, BLOCK), F32),
+        pltpu.VMEM((K, BLOCK), F32),
+        pltpu.VMEM((ITERS, NZ, 8, BLOCK), F32),
         pltpu.VMEM((ITERS, NZ, K, T), F32),
         pltpu.VMEM((ITERS, NZ, 1, BLOCK), F32),
         pltpu.VMEM((ITERS, NG, 1, BLOCK), F32),
@@ -496,13 +530,17 @@
         pltpu.VMEM((ITERS, NX, NY + 1, 8, BLOCK), F32),
         pltpu.VMEM((ITERS, NX, NY + 1, 8, BLOCK), F32),
         pltpu.VMEM((ITERS, NX, NY + 1, 8, BLOCK), F32),
-        pltpu.VMEM((ITERS, NY, 2, 8, BLOCK), F32),
-        pltpu.VMEM((ITERS, NY, 2, 8, BLOCK), F32),
+        pltpu.VMEM((ITERS, NY, 8, BLOCK), F32),
+        pltpu.VMEM((ITERS, NY, 8, BLOCK), F32),
+        pltpu.VMEM((ITERS, NY, 8, BLOCK), F32),
         pltpu.VMEM((ITERS, NC, NX, NY + 1, 8, BLOCK), F32),
         dma((NG,)),
+        dma((4,)),
     ]
-    for size in (NZ, NZ, NZ, NG, NY, NG, NY, NX, NX, NY, NY, NX, NX):
+    for size in (NZ, NZ, NZ, NG, NY, NG, NY, NX, NX, NY, NY, NY):
         scratch += [dma((ITERS, size)), dma((ITERS, size))]
+    for _ in range(2):
+        scratch += [dma((ITERS, NX, NY + 1)), dma((ITERS, NX, NY + 1))]
     basis, dark, coef = pl.pallas_call(
         functools.partial(fit_kernel, (NY, NX, NC, NZ, T, PX, K)),
         out_shape=(
@@ -510,11 +548,11 @@
             jax.ShapeDtypeStruct((1, PX), F32),
             jax.ShapeDtypeStruct((K, T), F32),
         ),
-        in_specs=[pl.BlockSpec(memory_space=pl.ANY), vmem, vmem, vmem, vmem],
+        in_specs=[pl.BlockSpec(memory_space=pl.ANY)] * 5,
         out_specs=(vmem, vmem, vmem),
         scratch_shapes=scratch,
         compiler_params=pltpu.CompilerParams(
-            collective_id=0, has_side_effects=True, vmem_limit_bytes=48 * 1024 * 1024
+            collective_id=0, has_side_effects=True, vmem_limit_bytes=67043328
         ),
     )(
         frames,

time: 114 us -> 111 us (0.974)
  local copies, waits for them, and re-layouts: 6.52 us -> 4.32 us
    unnamed x13 -> x3, local copies, waits for them, and re-layouts: 6.52 us -> 4.32 us
where the time goes in v2:
time: 111 us
  Pallas kernels  106 us (95%)
  local copies, waits for them, and re-layouts  4.32 us (4%)
    pallas_call x1, Pallas kernels, local(): pl.pallas_call(functools.partial(fit_kernel, (NY, NX, NC, NZ, T, PX, K)),...  106 us
    unnamed x3, local copies, waits for them, and re-layouts  4.32 us

profile of v2, /device:TPU:1, one launch (start us, length us, event | category | flops | bytes accessed | tf_op | source)
XLA Modules:
  0.0 111.0 jit_solution(3856040489360312064)
XLA Ops:
  0.6 106.0 %shard_map.76 = (f32[16,4096]{1,0:T(8,128)}, f32[1,4096]{1,0:T(1,128)}, f32[16,256]{1,0:T(8,128)}) custom-call(bf16[256,4096]{1,0:T(8,128)(2,1)} %frames_hbm.1, s32[1,256]{1,0:T(1,128)} %bitcast.8, s32[1,256]{1,0:T(1,128)} %bitcast.9, f32[16,4096]{1,0:T(8,128)} %basis_hbm.1, f32[1,4096]{1,0:T(1,128)} %bitcast.5), custom_call_target="tpu_custom_call" | custom-call | tf_op jit(solution)/shard_map/pallas_call | solution.py:544
  106.7 1.7 %copy.11 = f32[16,4096]{1,0:T(8,128)} copy(f32[16,4096]{1,0:T(8,128)} %get-tuple-element.12) | data formatting | bytes 524288
  108.3 1.3 %copy.12 = f32[4096]{0:T(1024)} copy(f32[4096]{0:T(1024)} %bitcast.7) | data formatting | bytes 32768
  109.7 1.3 %copy.13 = f32[256,16]{0,1:T(8,128)} copy(f32[256,16]{0,1:T(8,128)} %bitcast.6) | data formatting | bytes 32768

commit v3 on v2

--- a/solution.py
+++ b/solution.py
@@ -11,6 +11,7 @@
 ROW_PX = 2048
 BLOCK = 128
 ITERS = 2
+FORE_MAX = 8
 TILES = ("tiles_0", "tiles_1", "tiles_2")
 MESH = pl.DeviceIdType.MESH
 HIGHEST = lax.Precision.HIGHEST
@@ -38,6 +39,11 @@
         col = a[:, k : k + 1]
         a = jnp.where(sub == k, row, jnp.where(lane == k, 0.0, a) - col * row)
     return a
+
+
+def cuts_of(NY):
+    half = NY // 2 + 1
+    return [(0, half), (half, NY + 1)]
 
 
 def fit_kernel(
@@ -58,6 +64,8 @@
     coef_lhs,
     term_lhs,
     limit,
+    spot,
+    floats,
     masked,
     fold,
     gram_z,
@@ -158,6 +166,17 @@
                 barrier, inc=1, device_id=dev(lax.rem(me + o, size)), device_id_type=MESH
             )
 
+    near_y = sorted(range(1, NY), key=lambda o: min(o, NY - o))
+    near_x = sorted(range(1, NX), key=lambda o: min(o, NX - o))
+    slots = {0: 0, **{o: i + 1 for i, o in enumerate(near_y)}}
+    cuts = cuts_of(NY)
+
+    def slot_of(tile):
+        o = lax.rem(tile - y + NY, NY)
+        behind = o // (NY // 2 + 1)
+        own = (NY - o) // NY
+        return (1 - behind) * (2 * o - 1 + own) + behind * (2 * NY - 2 * o)
+
     sent = []
 
     def copy(src, dst, ssem, rsem, dev):
@@ -190,20 +209,27 @@
             total = total + buf[i]
         return total
 
-    small[0].wait()
-    small[1].wait()
-    valid_row = valid_ref[...].astype(F32)
-    limit_row = jnp.where(valid_ref[...] > 0, fore_ref[...].astype(F32), 1000.0)
-    limit[...] = jnp.broadcast_to(limit_row, (BLOCK, T)).T
-
     kinds = ROW_PX // BLOCK
-    for k in range(kinds):
-        masked[k : k + 1, :] = jnp.sum(
-            jnp.where(limit[...] > float(k), 1.0, 0.0), axis=0, keepdims=True
-        )
 
     def kind_of(block):
         return lax.rem(z * (NG * NB) + block, kinds)
+
+    def tables():
+        small[0].wait()
+        small[1].wait()
+        valid_row = valid_ref[...].astype(F32)
+        limit[...] = jnp.broadcast_to(fore_ref[...].astype(F32), (BLOCK, T)).T
+        valid_tiles = jnp.broadcast_to(valid_row, (BLOCK, T)).T
+        bad = 1.0 - valid_tiles
+        for k in range(kinds):
+            out = bad if k >= FORE_MAX else jnp.where(limit[...] > float(k), 1.0, bad)
+            masked[k : k + 1, :] = jnp.sum(out, axis=0, keepdims=True)
+        spot[...] = valid_tiles
+
+        @pl.loop(0, NG * NB)
+        def _(b):
+            cols = pl.ds(pl.multiple_of(b * BLOCK, BLOCK), BLOCK)
+            floats[:, cols] = frames[:, cols].astype(F32) * spot[...]
 
     row16 = lax.broadcasted_iota(jnp.int32, (16, GW), 0)
 
@@ -264,6 +290,8 @@
         proj_z[it, pl.ds(z, 1)] = (proj[:K] + proj[K:])[None]
         to_all(at(proj_z), at(s_proj), at(r_proj), NZ, z, z_dev)
 
+        if it == 0:
+            tables()
         from_all(at(gram_z), at(s_gram), at(r_gram), NZ, z, z_dev)
         folded = summed(at(gram_z), NZ)
         raw = jnp.concatenate([folded, pltpu.roll(folded, BLOCK // 2, 1)], axis=0)
@@ -280,35 +308,38 @@
         if last:
             coef_out[...] = coef
 
-        cg = lax.dot_general(
-            coef * valid_row, coef, NT, precision=HIGHEST, preferred_element_type=F32
-        )
-        cg_g[it, pl.ds(gi, 1), :, :K] = cg[None]
-        to_all(at(cg_g), at(s_cgg), at(r_cgg), NG, gi, g_dev)
-
+        valid_row = valid_ref[...].astype(F32)
         c_high = coef.astype(BF16).astype(F32)
         c_stack = jnp.concatenate(
             [c_high, c_high, coef - c_high, jnp.ones((K, T), F32)], axis=0
         )
-        coef_lhs[...] = c_stack.T.astype(BF16)
-
-        def residual(g, acc):
-            cols = cols_of(g)
-            fitted = lax.dot_general(
-                coef_lhs[...], stack[:, cols], NN, preferred_element_type=F32
-            )
-            r = frames[:, cols].astype(F32) - fitted
-            for j in range(NB):
-                kind = kind_of(g * NB + j).astype(F32)
-                rj = jnp.where(limit[...] <= kind, r[:, j * BLOCK : (j + 1) * BLOCK], 0.0)
-                resid[:, pl.ds(pl.multiple_of(g * GW + j * BLOCK, BLOCK), BLOCK)] = rj
-                acc = acc + jnp.sum((rj * rj).reshape(T // 8, 8, BLOCK), axis=0)
+        coef_lhs[...] = (c_stack * valid_row).T.astype(BF16)
+
+        aligned = (NX * NB) % kinds == 0
+
+        def residual(cc, acc):
+            for b in range(NX * NB):
+                block = cc * (NX * NB) + b
+                cols = pl.ds(pl.multiple_of(block * BLOCK, BLOCK), BLOCK)
+                r = floats[:, cols] - lax.dot_general(
+                    coef_lhs[...], stack[:, cols], NN, preferred_element_type=F32
+                )
+                kind = b % kinds if aligned else kind_of(block).astype(F32)
+                if not aligned or kind < FORE_MAX:
+                    r = jnp.where(limit[...] <= kind, r, 0.0)
+                resid[:, cols] = r
+                acc = acc + jnp.sum((r * r).reshape(T // 8, 8, BLOCK), axis=0)
             return acc
 
-        acc = lax.fori_loop(0, NG, residual, jnp.zeros((8, BLOCK), F32))
+        acc = lax.fori_loop(0, NC, residual, jnp.zeros((8, BLOCK), F32))
         sq_z[it, pl.ds(z, 1)] = jnp.sum(acc, axis=0, keepdims=True)[None]
         to_all(at(sq_z), at(s_sqz), at(r_sqz), NZ, z, z_dev)
 
+        cg = lax.dot_general(
+            coef * valid_row, coef, NT, precision=HIGHEST, preferred_element_type=F32
+        )
+        cg_g[it, pl.ds(gi, 1), :, :K] = cg[None]
+        to_all(at(cg_g), at(s_cgg), at(r_cgg), NG, gi, g_dev)
         from_all(at(cg_g), at(s_cgg), at(r_cgg), NG, gi, g_dev)
         cg_y[it, pl.ds(y, 1)] = summed(at(cg_g), NG)[None]
         to_all(at(cg_y), at(s_cgy), at(r_cgy), NY, y, y_dev)
@@ -336,19 +367,32 @@
 
         def terms(cc, xx):
             g = cc * NX + xx
-            for j in range(NB):
-                cols = pl.ds(pl.multiple_of(g * GW + j * BLOCK, BLOCK), BLOCK)
-                r = resid[:, cols]
-                w = 1.0 / (1.0 + r * r * rate)
-                wr = w * r
+            pair = min(2, NB)
+            for first in range(0, NB, pair):
+                sides = []
+                for j in range(first, first + pair):
+                    cols = pl.ds(pl.multiple_of(g * GW + j * BLOCK, BLOCK), BLOCK)
+                    r = resid[:, cols]
+                    w = 1.0 / (1.0 + r * r * rate)
+                    wr = w * r
+                    sides.append(wr.astype(BF16))
+                    part[it, cc, xx, NY, 2 * j : 2 * j + 1, :] = jnp.sum(
+                        wr, axis=0, keepdims=True
+                    )
+                    part[it, cc, xx, NY, 2 * j + 1 : 2 * j + 2, :] = (
+                        jnp.sum(w, axis=0, keepdims=True)
+                        - masked[pl.ds(kind_of(g * NB + j), 1), :]
+                    )
                 a = lax.dot_general(
-                    term_lhs[...], wr.astype(BF16), NN, preferred_element_type=F32
+                    term_lhs[...],
+                    jnp.concatenate(sides, axis=1),
+                    NN,
+                    preferred_element_type=F32,
                 )
-                part[it, cc, xx, pl.ds(2 * j, 2)] = (a[:K] + a[K:]).reshape(2, 8, BLOCK)
-                part[it, cc, xx, NY, 2 * j : 2 * j + 1, :] = jnp.sum(wr, axis=0, keepdims=True)
-                part[it, cc, xx, NY, 2 * j + 1 : 2 * j + 2, :] = (
-                    jnp.sum(w, axis=0, keepdims=True) - masked[pl.ds(kind_of(g * NB + j), 1), :]
-                )
+                a = a[:K] + a[K:]
+                for j in range(first, first + pair):
+                    tile = a[:, (j - first) * BLOCK : (j - first + 1) * BLOCK]
+                    part[it, cc, xx, pl.ds(2 * j, 2)] = tile.reshape(2, 8, BLOCK)
 
         def core_copy(xx):
             return copy(
@@ -364,26 +408,20 @@
                 x_src.at[it, xx], x_in.at[it, x], s_x.at[it, xx], r_x.at[it, x], x_dev(xx)
             )
 
-        @pl.loop(0, NX)
-        def _(i):
-            xx = lax.rem(x + 1 + i, NX)
+        order_x = list(reversed(near_x))
+        for o in [*order_x, 0]:
+            xx = lax.rem(x + o, NX)
             terms(other, xx)
             core_copy(xx).start()
-
-        @pl.loop(0, NX)
-        def _(i):
-            xx = lax.rem(x + 1 + i, NX)
+        for o in [*order_x, 0]:
+            xx = lax.rem(x + o, NX)
             terms(c, xx)
             core_copy(xx).wait_recv()
             both = part[it, c, xx] + from_core[it, xx]
-
-            @pl.when(i < NX - 1)
-            def _():
+            if o:
                 x_src[it, xx] = both
                 x_copy(xx).start()
-
-            @pl.when(i == NX - 1)
-            def _():
+            else:
                 x_in[it, x] = both
 
         for o in range(1, NX):
@@ -392,8 +430,6 @@
                 x_src.at[it, src], x_in.at[it, src], s_x.at[it, src], r_x.at[it, src], x_dev(src)
             ).wait_recv()
         mine = summed(at(x_in), NX)
-        near_y = sorted(range(1, NY), key=lambda o: min(o, NY - o))
-        near_x = sorted(range(1, NX), key=lambda o: min(o, NX - o))
         y_src[it] = mine[:NY]
         sum_in[it, y] = mine[NY]
         y_in[it, y] = y_src[it, y]
@@ -406,53 +442,54 @@
             copy(
                 y_src.at[it, src], y_in.at[it, src], s_y.at[it, o], r_y.at[it, src], y_dev(src)
             ).wait_recv()
-        full[it, c, x, y] = summed(at(y_in), NY)
-
-        def tile_copy(xx, tile, dev, ssem, rsem):
-            where = full.at[it, c, xx, tile]
+        full[it, c, x, 0] = summed(at(y_in), NY)
+
+        def chunk_copy(xx, cut, dev, ssem, rsem):
+            low, high = cuts[cut]
+            where = full.at[it, c, xx, pl.ds(low, high - low)]
             return copy(where, where, ssem, rsem, dev)
 
         def begin(made):
             made.start()
             sent.append(made)
 
-        def onward(tile):
+        def to_core(xx, cut):
+            begin(chunk_copy(xx, cut, c_dev(), s_ca.at[it, xx, cut], r_ca.at[it, xx, cut]))
+
+        def onward(cut):
             for o in reversed(near_x):
-                begin(
-                    tile_copy(
-                        x,
-                        tile,
-                        x_dev(lax.rem(x + o, NX)),
-                        s_xa.at[it, o, tile],
-                        r_xa.at[it, x, tile],
-                    )
-                )
-            to_core(x, tile)
-
-        def to_core(xx, tile):
-            begin(
-                tile_copy(xx, tile, c_dev(), s_ca.at[it, xx, tile], r_ca.at[it, xx, tile])
+                dev = x_dev(lax.rem(x + o, NX))
+                begin(chunk_copy(x, cut, dev, s_xa.at[it, o, cut], r_xa.at[it, x, cut]))
+            to_core(x, cut)
+
+        def y_gather(o, yy, slot):
+            return copy(
+                full.at[it, c, x, 0],
+                full.at[it, c, x, slot],
+                s_ya.at[it, o],
+                r_ya.at[it, slot],
+                y_dev(yy),
             )
 
         for o in reversed(near_y):
-            begin(
-                tile_copy(x, y, y_dev(lax.rem(y + o, NY)), s_ya.at[it, o], r_ya.at[it, y])
-            )
-        onward(y)
-        from_all(at(sum_in), at(s_t), at(r_t), NY, y, y_dev)
-        full[it, c, x, NY] = summed(at(sum_in), NY)
-        onward(NY)
-        for o in near_y:
-            src = lax.rem(y + o, NY)
-            tile_copy(x, src, y_dev(src), s_ya.at[it, o], r_ya.at[it, src]).wait_recv()
-            onward(src)
+            begin(y_gather(o, lax.rem(y + o, NY), slots[NY - o]))
+        for cut, (low, high) in enumerate(cuts):
+            if high == NY + 1:
+                from_all(at(sum_in), at(s_t), at(r_t), NY, y, y_dev)
+                full[it, c, x, NY] = summed(at(sum_in), NY)
+            for o in near_y:
+                if low <= slots[o] < high:
+                    y_gather(o, lax.rem(y + o, NY), slots[o]).wait_recv()
+            onward(cut)
 
         def apply(cc, xx):
             g = cc * NX + xx
             for j in range(NB):
                 cols = pl.ds(pl.multiple_of(g * GW + j * BLOCK, BLOCK), BLOCK)
-                delta = full[it, cc, xx, pl.ds(2 * j, 2)].reshape(K, BLOCK)
-                basis_out[:, cols] = basis_out[:, cols] + delta
+                for half in range(2):
+                    rows = pl.ds(8 * half, 8)
+                    delta = full[it, cc, xx, slot_of(2 * j + half)]
+                    basis_out[rows, cols] = basis_out[rows, cols] + delta
                 top = full[it, cc, xx, NY, 2 * j : 2 * j + 1, :]
                 low = full[it, cc, xx, NY, 2 * j + 1 : 2 * j + 2, :]
                 dark_out[:, cols] = dark_out[:, cols] + top / (low + 1.0)
@@ -467,28 +504,24 @@
 
         carry = 0 if last else (gram0, proj0)
         carry = take(c, x, carry)
-        for tile in [y, NY] + [lax.rem(y + o, NY) for o in near_y]:
+        for cut in range(len(cuts)):
             for o in near_x:
                 src = lax.rem(x + o, NX)
-                tile_copy(
-                    src, tile, x_dev(src), s_xa.at[it, o, tile], r_xa.at[it, src, tile]
+                chunk_copy(
+                    src, cut, x_dev(src), s_xa.at[it, o, cut], r_xa.at[it, src, cut]
                 ).wait_recv()
-                to_core(src, tile)
-
-        def own(i, carry):
-            return take(c, lax.rem(x + i, NX), carry)
-
-        def partner(i, carry):
-            xx = lax.rem(x + i, NX)
-            for tile in range(NY + 1):
-                where = full.at[it, other, xx, tile]
+                to_core(src, cut)
+
+        for o in near_x:
+            carry = take(c, lax.rem(x + o, NX), carry)
+        for o in [0, *near_x]:
+            xx = lax.rem(x + o, NX)
+            for cut, (low, high) in enumerate(cuts):
+                where = full.at[it, other, xx, pl.ds(low, high - low)]
                 copy(
-                    where, where, s_ca.at[it, xx, tile], r_ca.at[it, xx, tile], c_dev()
+                    where, where, s_ca.at[it, xx, cut], r_ca.at[it, xx, cut], c_dev()
                 ).wait_recv()
-            return take(other, xx, carry)
-
-        carry = lax.fori_loop(1, NX, own, carry)
-        carry = lax.fori_loop(0, NX, partner, carry)
+            carry = take(other, xx, carry)
         if not last:
             gram, proj = carry
 
@@ -499,6 +532,14 @@
 
     for made in sent:
         made.wait_send()
+
+
+def write_kernel(*refs):
+    copies = [pltpu.make_async_copy(refs[i], refs[i + 3], refs[6].at[i]) for i in range(3)]
+    for made in copies:
+        made.start()
+    for made in copies:
+        made.wait()
 
 
 def local(frames, tile_valid, foreground_blocks, basis_start, dark_start):
@@ -517,6 +558,8 @@
         pltpu.VMEM((T, 4 * K), BF16),
         pltpu.VMEM((2 * K, T), BF16),
         pltpu.VMEM((T, BLOCK), F32),
+        pltpu.VMEM((T, BLOCK), F32),
+        pltpu.VMEM((T, PX), F32),
         pltpu.VMEM((ROW_PX // BLOCK, BLOCK), F32),
         pltpu.VMEM((K, BLOCK), F32),
         pltpu.VMEM((ITERS, NZ, 8, BLOCK), F32),
@@ -540,7 +583,7 @@
     for size in (NZ, NZ, NZ, NG, NY, NG, NY, NX, NX, NY, NY, NY):
         scratch += [dma((ITERS, size)), dma((ITERS, size))]
     for _ in range(2):
-        scratch += [dma((ITERS, NX, NY + 1)), dma((ITERS, NX, NY + 1))]
+        scratch += [dma((ITERS, NX, len(cuts_of(NY)))), dma((ITERS, NX, len(cuts_of(NY))))]
     basis, dark, coef = pl.pallas_call(
         functools.partial(fit_kernel, (NY, NX, NC, NZ, T, PX, K)),
         out_shape=(
@@ -552,7 +595,7 @@
         out_specs=(vmem, vmem, vmem),
         scratch_shapes=scratch,
         compiler_params=pltpu.CompilerParams(
-            collective_id=0, has_side_effects=True, vmem_limit_bytes=67043328
+            collective_id=0, has_side_effects=True, vmem_limit_bytes=67043328 - 65536
         ),
     )(
         frames,
@@ -561,6 +604,14 @@
         basis_start,
         dark_start.reshape(1, PX),
     )
+    results = (basis, dark, coef)
+    basis, dark, coef = pl.pallas_call(
+        write_kernel,
+        out_shape=tuple(jax.ShapeDtypeStruct(r.shape, r.dtype) for r in results),
+        in_specs=[vmem] * 3,
+        out_specs=[pl.BlockSpec(memory_space=pltpu.HBM)] * 3,
+        scratch_shapes=[dma((3,))],
+    )(*results)
     return basis, dark.reshape(PX), coef.T
 
 

time: 111 us -> 104 us (0.937)
  local copies, waits for them, and re-layouts: 4.32 us -> 0 us
  Pallas kernels: 106 us -> 103 us
    pallas_call x1, Pallas kernels: 106 us -> 101 us  [local(): pl.pallas_call(functools.partial(fit_kernel, (NY, NX, NC, NZ, T, PX, K)),...]
    unnamed x3 -> x0, local copies, waits for them, and re-layouts: 4.32 us -> none
    pallas_call x0 -> x1, Pallas kernels: none -> 1.7 us  [local(): pl.pallas_call(write_kernel, out_shape=tuple((jax.ShapeDtypeStruct(r.shap...]
where the time goes in v3:
time: 104 us
  Pallas kernels  103 us (99%)
    pallas_call x1, Pallas kernels, local(): pl.pallas_call(functools.partial(fit_kernel, (NY, NX, NC, NZ, T, PX, K)),...  101 us

profile of v3, /device:TPU:1, one launch (start us, length us, event | category | flops | bytes accessed | tf_op | source)
XLA Modules:
  0.0 103.8 jit_solution(2679691559602062028)
XLA Ops:
  0.6 101.4 %shard_map.76 = (f32[16,4096]{1,0:T(8,128)}, f32[1,4096]{1,0:T(1,128)}, f32[16,256]{1,0:T(8,128)}) custom-call(bf16[256,4096]{1,0:T(8,128)(2,1)} %frames_hbm.1, s32[1,256]{1,0:T(1,128)} %bitcast.6, s32[1,256]{1,0:T(1,128)} %bitcast.7, f32[16,4096]{1,0:T(8,128)} %basis_hbm.1, f32[1,4096]{1,0:T(1,128)} %bitcast.5), custom_call_target="tpu_custom_call" | custom-call | tf_op jit(solution)/shard_map/pallas_call | solution.py:587
  102.1 1.7 %shard_map.77 = (f32[16,4096]{1,0:T(8,128)}, f32[1,4096]{1,0:T(1,128)}, f32[16,256]{1,0:T(8,128)}) custom-call(f32[16,4096]{1,0:T(8,128)} %get-tuple-element.9.refs_0_, f32[1,4096]{1,0:T(1,128)} %get-tuple-element.10.refs_1_, f32[16,256]{1,0:T(8,128)} %get-tuple-element.11.refs_2_), custom_call_target="tpu_custom_call" | custom-call | tf_op jit(solution)/shard_map/pallas_call | solution.py:608

commit v4 on v3

--- a/solution.py
+++ b/solution.py
@@ -189,19 +189,17 @@
             device_id_type=MESH,
         )
 
-    def start(*args):
-        made = copy(*args)
-        made.start()
-        sent.append(made)
+    def whole(buf, ssem, rsem, size, me, dev):
+        every = buf.at[pl.ds(0, size - 1)]
+        return copy(every, every, ssem, rsem, dev(lax.rem(me + 1, size)))
 
     def to_all(buf, ssem, rsem, size, me, dev):
         for o in range(1, size):
-            start(buf.at[me], buf.at[me], ssem.at[o], rsem.at[me], dev(lax.rem(me + o, size)))
+            copy(buf.at[me], buf.at[me], ssem, rsem, dev(lax.rem(me + o, size))).start()
+        sent.append(whole(buf, ssem, rsem, size, me, dev))
 
     def from_all(buf, ssem, rsem, size, me, dev):
-        for o in range(1, size):
-            src = lax.rem(me + o, size)
-            copy(buf.at[src], buf.at[src], ssem.at[o], rsem.at[src], dev(src)).wait_recv()
+        whole(buf, ssem, rsem, size, me, dev).wait_recv()
 
     def summed(buf, size):
         total = buf[0]
@@ -398,14 +396,14 @@
             return copy(
                 part.at[it, other, xx],
                 from_core.at[it, xx],
-                s_core.at[it, xx],
+                s_core.at[it],
                 r_core.at[it, xx],
                 c_dev(),
             )
 
         def x_copy(xx):
             return copy(
-                x_src.at[it, xx], x_in.at[it, x], s_x.at[it, xx], r_x.at[it, x], x_dev(xx)
+                x_src.at[it, xx], x_in.at[it, x], s_x.at[it], r_x.at[it], x_dev(xx)
             )
 
         order_x = list(reversed(near_x))
@@ -424,24 +422,16 @@
             else:
                 x_in[it, x] = both
 
-        for o in range(1, NX):
-            src = lax.rem(x + o, NX)
-            copy(
-                x_src.at[it, src], x_in.at[it, src], s_x.at[it, src], r_x.at[it, src], x_dev(src)
-            ).wait_recv()
+        from_all(at(x_in), at(s_x), at(r_x), NX, x, x_dev)
         mine = summed(at(x_in), NX)
         y_src[it] = mine[:NY]
         sum_in[it, y] = mine[NY]
         y_in[it, y] = y_src[it, y]
         for o in reversed(near_y):
             yy = lax.rem(y + o, NY)
-            start(y_src.at[it, yy], y_in.at[it, y], s_y.at[it, o], r_y.at[it, y], y_dev(yy))
+            copy(y_src.at[it, yy], y_in.at[it, y], at(s_y), at(r_y), y_dev(yy)).start()
         to_all(at(sum_in), at(s_t), at(r_t), NY, y, y_dev)
-        for o in near_y:
-            src = lax.rem(y + o, NY)
-            copy(
-                y_src.at[it, src], y_in.at[it, src], s_y.at[it, o], r_y.at[it, src], y_dev(src)
-            ).wait_recv()
+        from_all(at(y_in), at(s_y), at(r_y), NY, y, y_dev)
         full[it, c, x, 0] = summed(at(y_in), NY)
 
         def chunk_copy(xx, cut, dev, ssem, rsem):
@@ -449,37 +439,33 @@
             where = full.at[it, c, xx, pl.ds(low, high - low)]
             return copy(where, where, ssem, rsem, dev)
 
-        def begin(made):
-            made.start()
-            sent.append(made)
-
         def to_core(xx, cut):
-            begin(chunk_copy(xx, cut, c_dev(), s_ca.at[it, xx, cut], r_ca.at[it, xx, cut]))
+            chunk_copy(xx, cut, c_dev(), s_ca.at[it], r_ca.at[it, xx]).start()
 
         def onward(cut):
             for o in reversed(near_x):
                 dev = x_dev(lax.rem(x + o, NX))
-                begin(chunk_copy(x, cut, dev, s_xa.at[it, o, cut], r_xa.at[it, x, cut]))
+                chunk_copy(x, cut, dev, s_xa.at[it], r_xa.at[it, cut]).start()
             to_core(x, cut)
 
-        def y_gather(o, yy, slot):
-            return copy(
+        for o in reversed(near_y):
+            slot = slots[NY - o]
+            cut = [low <= slot < high for low, high in cuts].index(True)
+            copy(
                 full.at[it, c, x, 0],
                 full.at[it, c, x, slot],
-                s_ya.at[it, o],
-                r_ya.at[it, slot],
-                y_dev(yy),
-            )
-
-        for o in reversed(near_y):
-            begin(y_gather(o, lax.rem(y + o, NY), slots[NY - o]))
+                s_ya.at[it],
+                r_ya.at[it, cut],
+                y_dev(lax.rem(y + o, NY)),
+            ).start()
         for cut, (low, high) in enumerate(cuts):
             if high == NY + 1:
                 from_all(at(sum_in), at(s_t), at(r_t), NY, y, y_dev)
                 full[it, c, x, NY] = summed(at(sum_in), NY)
-            for o in near_y:
-                if low <= slots[o] < high:
-                    y_gather(o, lax.rem(y + o, NY), slots[o]).wait_recv()
+            count = sum(low <= slots[o] < high for o in near_y)
+            if count:
+                some = full.at[it, c, x, pl.ds(0, count)]
+                copy(some, some, s_ya.at[it], r_ya.at[it, cut], y_dev(lax.rem(y + 1, NY))).wait_recv()
             onward(cut)
 
         def apply(cc, xx):
@@ -504,31 +490,31 @@
 
         carry = 0 if last else (gram0, proj0)
         carry = take(c, x, carry)
-        for cut in range(len(cuts)):
-            for o in near_x:
-                src = lax.rem(x + o, NX)
-                chunk_copy(
-                    src, cut, x_dev(src), s_xa.at[it, o, cut], r_xa.at[it, src, cut]
-                ).wait_recv()
-                to_core(src, cut)
+        for cut, (low, high) in enumerate(cuts):
+            some = full.at[it, c, pl.ds(0, NX - 1), pl.ds(low, high - low)]
+            copy(some, some, s_xa.at[it], r_xa.at[it, cut], x_dev(lax.rem(x + 1, NX))).wait_recv()
+            for o in reversed(near_x):
+                to_core(lax.rem(x + o, NX), cut)
 
         for o in near_x:
             carry = take(c, lax.rem(x + o, NX), carry)
         for o in [0, *near_x]:
             xx = lax.rem(x + o, NX)
-            for cut, (low, high) in enumerate(cuts):
-                where = full.at[it, other, xx, pl.ds(low, high - low)]
-                copy(
-                    where, where, s_ca.at[it, xx, cut], r_ca.at[it, xx, cut], c_dev()
-                ).wait_recv()
+            where = full.at[it, other, xx]
+            copy(where, where, s_ca.at[it], r_ca.at[it, xx], c_dev()).wait_recv()
             carry = take(other, xx, carry)
         if not last:
             gram, proj = carry
 
-        for xx in range(NX):
-            core_copy(xx).wait_send()
-        for o in range(1, NX):
-            x_copy(lax.rem(x + o, NX)).wait_send()
+        for ref, sem in (
+            (part.at[it, c], s_core),
+            (x_src.at[it, pl.ds(0, NX - 1)], s_x),
+            (y_src.at[it, pl.ds(0, NY - 1)], s_y),
+            (full.at[it, c, x, pl.ds(0, NY - 1)], s_ya),
+            (full.at[it, c, pl.ds(0, NX - 1)], s_xa),
+            (full.at[it, c], s_ca),
+        ):
+            sent.append(copy(ref, ref, sem.at[it], r_core.at[it, 0], c_dev()))
 
     for made in sent:
         made.wait_send()
@@ -580,22 +566,21 @@
         dma((NG,)),
         dma((4,)),
     ]
-    for size in (NZ, NZ, NZ, NG, NY, NG, NY, NX, NX, NY, NY, NY):
-        scratch += [dma((ITERS, size)), dma((ITERS, size))]
-    for _ in range(2):
-        scratch += [dma((ITERS, NX, len(cuts_of(NY)))), dma((ITERS, NX, len(cuts_of(NY))))]
+    several = len(cuts_of(NY))
+    for arrivals in [()] * 7 + [(NX,)] + [()] * 3 + [(several,), (several,), (NX,)]:
+        scratch += [dma((ITERS,)), dma((ITERS, *arrivals))]
     basis, dark, coef = pl.pallas_call(
         functools.partial(fit_kernel, (NY, NX, NC, NZ, T, PX, K)),
         out_shape=(
-            jax.ShapeDtypeStruct((K, PX), F32),
-            jax.ShapeDtypeStruct((1, PX), F32),
-            jax.ShapeDtypeStruct((K, T), F32),
+            pltpu.VMEM((K, PX), F32),
+            pltpu.VMEM((1, PX), F32),
+            pltpu.VMEM((K, T), F32),
         ),
         in_specs=[pl.BlockSpec(memory_space=pl.ANY)] * 5,
         out_specs=(vmem, vmem, vmem),
         scratch_shapes=scratch,
         compiler_params=pltpu.CompilerParams(
-            collective_id=0, has_side_effects=True, vmem_limit_bytes=67043328 - 65536
+            collective_id=0, has_side_effects=True, vmem_limit_bytes=67043328 - 1400000
         ),
     )(
         frames,
@@ -608,9 +593,10 @@
     basis, dark, coef = pl.pallas_call(
         write_kernel,
         out_shape=tuple(jax.ShapeDtypeStruct(r.shape, r.dtype) for r in results),
-        in_specs=[vmem] * 3,
+        in_specs=[pl.BlockSpec(memory_space=pl.ANY)] * 3,
         out_specs=[pl.BlockSpec(memory_space=pltpu.HBM)] * 3,
         scratch_shapes=[dma((3,))],
+        compiler_params=pltpu.CompilerParams(vmem_limit_bytes=1024 * 1024),
     )(*results)
     return basis, dark.reshape(PX), coef.T
 

time: 104 us -> 99.2 us (0.954)
  Pallas kernels: 103 us -> 98.4 us
    pallas_call x1, Pallas kernels: 101 us -> 97.6 us  [local(): pl.pallas_call(functools.partial(fit_kernel, (NY, NX, NC, NZ, T, PX, K)),...]
where the time goes in v4:
time: 99.2 us; the launch traced here: 99 us
  Pallas kernels  98.4 us (99%)
    pallas_call x1, Pallas kernels, local(): pl.pallas_call(functools.partial(fit_kernel, (NY, NX, NC, NZ, T, PX, K)),...  97.6 us

profile of v4, /device:TPU:1, one launch (start us, length us, event | category | flops | bytes accessed | tf_op | source)
XLA Modules:
  0.0 99.0 jit_solution(12367366822573265002)
XLA Ops:
  0.6 97.6 %shard_map.76 = (f32[16,4096]{1,0:T(8,128)S(1)}, f32[1,4096]{1,0:T(1,128)S(1)}, f32[16,256]{1,0:T(8,128)S(1)}) custom-call(bf16[256,4096]{1,0:T(8,128)(2,1)} %frames_hbm.1, s32[1,256]{1,0:T(1,128)} %bitcast.6, s32[1,256]{1,0:T(1,128)} %bitcast.7, f32[16,4096]{1,0:T(8,128)} %basis_hbm.1, f32[1,4096]{1,0:T(1,128)} %bitcast.5), custom_call_target="tpu_custom_call" | custom-call | tf_op jit(solution)/shard_map/pallas_call | solution.py:572
  98.3 0.7 shard_map.77

commit v5 on v4

--- a/solution.py
+++ b/solution.py
@@ -194,7 +194,7 @@
         return copy(every, every, ssem, rsem, dev(lax.rem(me + 1, size)))
 
     def to_all(buf, ssem, rsem, size, me, dev):
-        for o in range(1, size):
+        for o in sorted(range(1, size), key=lambda o: -min(o, size - o)):
             copy(buf.at[me], buf.at[me], ssem, rsem, dev(lax.rem(me + o, size))).start()
         sent.append(whole(buf, ssem, rsem, size, me, dev))
 
@@ -361,7 +361,7 @@
         from_all(at(sq_y), at(s_sqy), at(r_sqy), NY, y, y_dev)
         square = jnp.sum(summed(at(sq_y), NY), axis=1, keepdims=True)
         spread = square / (float(tiles_all) * float(pixels_all)) + 1e-05
-        rate = 1.0 / (4.0 * spread)
+        knee = 4.0 * spread
 
         def terms(cc, xx):
             g = cc * NX + xx
@@ -371,14 +371,14 @@
                 for j in range(first, first + pair):
                     cols = pl.ds(pl.multiple_of(g * GW + j * BLOCK, BLOCK), BLOCK)
                     r = resid[:, cols]
-                    w = 1.0 / (1.0 + r * r * rate)
+                    w = 1.0 / (knee + r * r)
                     wr = w * r
                     sides.append(wr.astype(BF16))
-                    part[it, cc, xx, NY, 2 * j : 2 * j + 1, :] = jnp.sum(
+                    part[it, cc, xx, NY, 2 * j : 2 * j + 1, :] = knee * jnp.sum(
                         wr, axis=0, keepdims=True
                     )
                     part[it, cc, xx, NY, 2 * j + 1 : 2 * j + 2, :] = (
-                        jnp.sum(w, axis=0, keepdims=True)
+                        knee * jnp.sum(w, axis=0, keepdims=True)
                         - masked[pl.ds(kind_of(g * NB + j), 1), :]
                     )
                 a = lax.dot_general(
@@ -387,7 +387,7 @@
                     NN,
                     preferred_element_type=F32,
                 )
-                a = a[:K] + a[K:]
+                a = knee * (a[:K] + a[K:])
                 for j in range(first, first + pair):
                     tile = a[:, (j - first) * BLOCK : (j - first + 1) * BLOCK]
                     part[it, cc, xx, pl.ds(2 * j, 2)] = tile.reshape(2, 8, BLOCK)

time: 99.2 us -> 97.8 us (0.986)
  Pallas kernels: 98.4 us -> 97 us
    pallas_call x1, Pallas kernels: 97.6 us -> 96.3 us  [local(): pl.pallas_call(functools.partial(fit_kernel, (NY, NX, NC, NZ, T, PX, K)),...]
where the time goes in v5:
time: 97.8 us; the launch traced here: 97.7 us
  Pallas kernels  97 us (99%)
    pallas_call x1, Pallas kernels, local(): pl.pallas_call(functools.partial(fit_kernel, (NY, NX, NC, NZ, T, PX, K)),...  96.3 us

profile of v5, /device:TPU:1, one launch (start us, length us, event | category | flops | bytes accessed | tf_op | source)
XLA Modules:
  0.0 97.7 jit_solution(3223521468264460694)
XLA Ops:
  0.6 96.3 %shard_map.76 = (f32[16,4096]{1,0:T(8,128)S(1)}, f32[1,4096]{1,0:T(1,128)S(1)}, f32[16,256]{1,0:T(8,128)S(1)}) custom-call(bf16[256,4096]{1,0:T(8,128)(2,1)} %frames_hbm.1, s32[1,256]{1,0:T(1,128)} %bitcast.6, s32[1,256]{1,0:T(1,128)} %bitcast.7, f32[16,4096]{1,0:T(8,128)} %basis_hbm.1, f32[1,4096]{1,0:T(1,128)} %bitcast.5), custom_call_target="tpu_custom_call" | custom-call | tf_op jit(solution)/shard_map/pallas_call | solution.py:572
  97.0 0.7 shard_map.77
